TPU v7x, 32 devices: a whole 2x2x4 slice. The times are simulated.
32 devices in a mesh: group: 2 (over y), lender: 4 (over z), tensor: 4 (over x, core).
Axes of the slice: x: 2, y: 2, z: 4, core: 2. Of those that a mesh axis runs over, the one named last changes fastest.
Arguments:
- activations: bfloat16 [16, 8192], P('group', 'lender'), parts along dimension 0, may hold values from -400 to 400
- norm_gain: bfloat16 [8192], P('lender'), may hold values from 0.099609375 to 1.8984375
- w_query: bfloat16 [8192, 8192], P('lender', 'tensor'), may hold values from -0.0625 to 0.0625
- w_out: bfloat16 [8192, 8192], P('tensor', 'lender'), may hold values from -0.0625 to 0.0625
- key_pool: bfloat16 [8, 256, 128, 128], P('tensor', ('group', 'lender')), parts along dimension 1, may hold values from -800 to 800
- value_block_store: bfloat16 [8, 256, 128, 128], P('tensor', ('group', 'lender')), parts along dimension 1, may hold values from -48 to 48
- block_list: int32 [16, 8, 16], P('group', 'tensor'), parts along dimension 0, may hold values from 0 to 127, as said below
- block_slot_table: int32 [8, 256], P('tensor', 'group'), parts along dimension 1, may hold values from 0 to 127, each once within a row
- kept_len: int32 [16, 8], P('group', 'tensor'), parts along dimension 0, may hold values from 1 to 16, as said below
Outputs:
- output: bfloat16 [16, 8192], P(('group', 'tensor'), 'lender'), parts along dimension 0
There are 2 independent parts, one for each index of `group`. A program takes and returns all parts, laid end to end along the dimension named above; an argument that names none is the same for every part. Nothing has to cross between parts.
Inputs may be any that keep to these rules, and one draw needn't show every extreme that they name: `block_list`: for each KV head, no logical block appears twice among all rows' lists. `kept_len`: some row of every KV head keeps 16 blocks and some other row keeps one.
All inputs are finite; a program needn't handle non-finite values.
Results may differ from a plain program's by a relative error of at most 0.012.
The roundings to bfloat16 on the way count: a program that leaves them out, or rounds other values in their place, can miss the bound.
Values may be sent and summed in bfloat16 or wider, within the bound.
No kernel may reach another device: no remote copies, remote signals or barrier semaphores. Data moves between devices by JAX's collectives and lax.ppermute only.
A program may use at most 64 MiB of HBM per device.

v0:
```python
import jax
import jax.numpy as jnp
from jax import lax
from jax.sharding import PartitionSpec as P

D = 8192


very_low = -1e30
epsilon = 1e-05


def per_device(
    activations,
    norm_gain,
    w_query,
    w_out,
    key_pool,
    value_block_store,
    block_list,
    block_slot_table,
    kept_len,
):
    row_count = activations.shape[0]
    kv_heads = key_pool.shape[0]
    slot_count = key_pool.shape[1]
    head_dim = key_pool.shape[3]
    kept_most = block_list.shape[2]
    features = activations.astype(jnp.float32)
    squares = jnp.sum(features * features, axis=1)
    scaled = (features * norm_gain.astype(jnp.float32)).astype(jnp.bfloat16)
    partial_value = jnp.dot(scaled, w_query, preferred_element_type=jnp.float32)
    projected, square_sum = lax.psum((partial_value, squares), "lender")
    inverse = lax.rsqrt(square_sum / D + epsilon)
    query_vectors = (projected * inverse[:, None] * head_dim ** (-0.5)).astype(jnp.bfloat16)
    group_size = query_vectors.shape[1] // (kv_heads * head_dim)
    query_vectors = query_vectors.reshape(row_count, kv_heads, group_size, head_dim)
    slot_lookup_table = jnp.broadcast_to(
        block_slot_table[None], (row_count,) + block_slot_table.shape
    )
    slot_ids = jnp.take_along_axis(slot_lookup_table, block_list, axis=2)
    positions = jnp.arange(kept_most, dtype=jnp.int32)
    is_live = positions[None, None, :] < kept_len[:, :, None]
    local_slot = slot_ids - lax.axis_index("lender") * slot_count
    matches = is_live[..., None] & (
        local_slot[..., None] == jnp.arange(slot_count, dtype=jnp.int32)
    )
    owner_mask = jnp.transpose(jnp.any(matches, axis=2), (1, 2, 0))
    owner_half = owner_mask.astype(jnp.bfloat16)
    owner_full = owner_mask.astype(jnp.float32)
    used_slot = jnp.any(owner_mask, axis=2)
    picked = jnp.einsum(
        "hsr,rhgd->hsgd", owner_half, query_vectors, preferred_element_type=jnp.float32
    ).astype(jnp.bfloat16)
    scores = jnp.einsum("hsgd,hstd->hsgt", picked, key_pool, preferred_element_type=jnp.float32)
    block_best = jnp.max(scores, axis=3)
    spread = jnp.where(owner_mask[..., None], block_best[:, :, None, :], very_low)
    row_best = jnp.max(spread, axis=1)
    slot_best = jnp.max(jnp.where(owner_mask[..., None], row_best[:, None, :, :], very_low), axis=2)
    slot_best = jnp.where(used_slot[..., None], slot_best, 0.0)
    weights_full = jnp.where(
        used_slot[:, :, None, None], jnp.exp(scores - slot_best[..., None]), 0.0
    )
    slot_weight = jnp.sum(weights_full, axis=3)
    slot_value = jnp.einsum(
        "hsgt,hstd->hsgd",
        weights_full.astype(jnp.bfloat16),
        value_block_store,
        preferred_element_type=jnp.float32,
    )
    row_weight = jnp.einsum(
        "hsr,hsg->rhg", owner_full, slot_weight, precision=lax.Precision.HIGHEST
    )
    row_value = jnp.einsum(
        "hsr,hsgd->rhgd", owner_full, slot_value, precision=lax.Precision.HIGHEST
    )
    row_high = jnp.transpose(row_best, (1, 0, 2))
    lenders = lax.axis_size("lender")
    home_rows = row_count // lenders
    came_best, came_weight, came_value = (
        lax.all_to_all(row_high, "lender", split_axis=0, concat_axis=0, tiled=True),
        lax.all_to_all(row_weight, "lender", split_axis=0, concat_axis=0, tiled=True),
        lax.all_to_all(row_value, "lender", split_axis=0, concat_axis=0, tiled=True),
    )
    came_best = came_best.reshape((lenders, home_rows) + came_best.shape[1:])
    came_weight = came_weight.reshape((lenders, home_rows) + came_weight.shape[1:])
    came_value = came_value.reshape((lenders, home_rows) + came_value.shape[1:])
    highest = jnp.max(came_best, axis=0)
    factor = jnp.exp(came_best - highest[None])
    home_weight = jnp.sum(came_weight * factor, axis=0)
    home_value = jnp.sum(came_value * factor[..., None], axis=0)
    home_attended = (
        (home_value / home_weight[..., None]).astype(jnp.bfloat16).reshape(home_rows, -1)
    )
    attended = lax.all_gather(home_attended, "lender", axis=0, tiled=True)
    result = lax.psum_scatter(
        jnp.dot(attended, w_out, preferred_element_type=jnp.float32),
        "tensor",
        scatter_dimension=0,
        tiled=True,
    )
    return result.astype(jnp.bfloat16)


def solution(mesh):
    in_specs = (
        P("group", "lender"),
        P("lender"),
        P("lender", "tensor"),
        P("tensor", "lender"),
        P("tensor", ("group", "lender"), None, None),
        P("tensor", ("group", "lender"), None, None),
        P("group", "tensor", None),
        P("tensor", "group"),
        P("group", "tensor"),
    )
    out_specs = P(("group", "tensor"), "lender")
    return jax.shard_map(
        per_device, mesh=mesh, in_specs=in_specs, out_specs=out_specs, check_vma=False
    )
```

profile of v0, /device:TPU:0, one launch (start us, length us, event | category | flops | bytes accessed | tf_op | source)
XLA Modules:
  0.0 116.3 jit_solution(14642296983015357791)
XLA Ops:
  6.5 0.0 copy-start
  6.5 0.0 all-reduce.3.cloned.1.call-start
  6.6 0.8 convert_element_type.31
  7.4 5.2 %fusion.15 = f32[8,2048]{1,0:T(8,128)} fusion(bf16[2048,2048]{1,0:T(8,128)(2,1)} %param.11, bf16[8,2048]{1,0:T(8,128)(2,1)} %param.9, f32[2048]{0:T(1024)S(1)} %convert_element_type.31), kind=kOutput, calls=%fused_computation.26 | convolution fusion | flops 67158016 | bytes 8495104 | tf_op jit(solution)/shard_map/dot_general | solution.py:32
  12.7 0.0 all-reduce.3.cloned.1.call-update
  12.7 0.0 copy-done.1
  12.7 0.1 fusion.13
  12.8 0.0 copy-done.2
  12.9 0.1 reshape.57
  12.9 0.0 copy-done.3
  13.0 2.6 %gather_fusion = s32[256]{0:T(256)S(1)} fusion(s32[8,2,128]{2,1,0:T(2,128)S(1)} %broadcast_in_dim.66, s32[256]{0:T(256)S(1)} %reshape.57), kind=kCustom, calls=%fused_computation | custom fusion | bytes 5120 | tf_op jit(solution)/shard_map/jit(take_along_axis)/gather | solution.py:41
  15.6 0.1 reshape.60
  15.6 0.0 copy-done.4
  15.7 0.1 copy.48
  15.7 0.1 iota_compare_fusion.1
  15.8 13.5 %psum.15 = f32[8]{0:T(128)S(1)} all-reduce(f32[8]{0:T(128)S(1)} %fusion.13), channel_id=1, replica_groups=mesh['group'=2,'lender'=4,'tensor'=4] {'lender'}, use_global_device_ids=true, to_apply=%region_4.5 | all-reduce | flops 8 | bytes 64 | tf_op jit(solution)/shard_map/psum | solution.py:33
  29.3 0.2 fusion.10
  29.5 0.0 copy-done.5
  29.5 0.6 dynamic-slice
  30.8 19.1 %all-reduce.3.cloned.1.call-done = f32[8,2048]{1,0:T(8,128)} async-done(((f32[8,2048]{1,0:T(8,128)}), f32[8,2048]{1,0:T(8,128)}) %all-reduce.3.cloned.1.call-update) | async-done | bytes 65552 | tf_op jit(solution)/shard_map/psum | solution.py:33
  49.9 0.9 multiply_convert_fusion
  50.8 0.2 convolution_convert_fusion
  51.1 1.3 %fusion.22 = (f32[2,32,8]{2,1,0:T(8,128)S(1)}, f32[2,32,8,128]{3,2,1,0:T(8,128)S(1)}) fusion(bf16[2,32,128,128]{3,2,1,0:T(8,128)(2,1)S(1)} %copy-done, bf16[2,32,8,128]{3,1,2,0:T(8,128)(2,1)S(1)} %convolution_convert_fusion), kind=kOutput, calls=%fused_computation.43 | convolution fusion | flops 16842240 | bytes 2492416 | tf_op jit(solution)/shard_map/hsgd,hstd->hsgt/dot_general | solution.py:55
  52.3 0.1 copy.52
  52.4 0.1 select_reduce_fusion.1
  52.5 0.1 select_reduce_fusion
  52.6 0.1 copy.53
  52.7 0.6 copy.57
  53.3 3.4 %all-to-all-start.1 = ((f32[8,2,8]{2,1,0:T(2,128)}), f32[8,2,8]{2,1,0:T(2,128)S(1)}, u32[]{:S(2)}, u32[]{:S(2)}) async-start(f32[8,2,8]{2,1,0:T(2,128)} %copy.57), calls=%async_computation.1 | async-start | bytes 16384 | tf_op jit(solution)/shard_map/all_to_all | solution.py:81
  56.7 0.3 fusion.1
  57.0 2.3 %fusion.3 = f32[2,32,8,128]{3,2,1,0:T(8,128)S(1)} fusion(bf16[2,32,128,128]{3,2,1,0:T(8,128)(2,1)} %param.14, f32[2,32,8,128]{3,2,1,0:T(8,128)S(1)} %get-tuple-element.8, f32[2,32,8]{2,1,0:T(8,128)S(1)} %copy.53, pred[2,32]{1,0:T(4,128)(4,1)S(1)} %bitcast_reduce_fusion), kind=kOutput, calls=%fused_computation.8 | convolution fusion | flops 16973824 | bytes 2623552 | tf_op jit(solution)/shard_map/hsgt,hstd->hsgd/dot_general | solution.py:65
  59.3 0.2 convolution_bitcast_fusion.1
  59.5 0.7 copy.63
  60.2 2.1 %all-to-all-done.1 = f32[8,2,8]{2,1,0:T(2,128)S(1)} async-done(((f32[8,2,8]{2,1,0:T(2,128)}), f32[8,2,8]{2,1,0:T(2,128)S(1)}, u32[]{:S(2)}, u32[]{:S(2)}) %all-to-all-start.1) | async-done | bytes 544 | tf_op jit(solution)/shard_map/all_to_all | solution.py:81
  62.3 3.2 %all-to-all-start.2 = ((f32[8,2,8]{2,1,0:T(2,128)}), f32[8,2,8]{2,1,0:T(2,128)S(1)}, u32[]{:S(2)}, u32[]{:S(2)}) async-start(f32[8,2,8]{2,1,0:T(2,128)} %copy.63), calls=%async_computation.2 | async-start | bytes 16384 | tf_op jit(solution)/shard_map/all_to_all | solution.py:82
  65.5 0.2 convolution_bitcast_fusion
  65.8 0.6 copy.56
  66.4 4.7 %all-to-all-done.2 = f32[8,2,8]{2,1,0:T(2,128)S(1)} async-done(((f32[8,2,8]{2,1,0:T(2,128)}), f32[8,2,8]{2,1,0:T(2,128)S(1)}, u32[]{:S(2)}, u32[]{:S(2)}) %all-to-all-start.2) | async-done | bytes 544 | tf_op jit(solution)/shard_map/all_to_all | solution.py:82
  71.1 3.3 %all-to-all-start = ((f32[8,2,8,128]{3,2,1,0:T(8,128)}), f32[8,2,8,128]{3,2,1,0:T(8,128)S(1)}, u32[]{:S(2)}, u32[]{:S(2)}) async-start(f32[8,2,8,128]{3,2,1,0:T(8,128)} %copy.56), calls=%async_computation | async-start | bytes 131072 | tf_op jit(solution)/shard_map/all_to_all | solution.py:83
  74.4 0.1 copy.59
  74.6 0.1 copy.65
  74.6 5.5 %all-to-all-done = f32[8,2,8,128]{3,2,1,0:T(8,128)S(1)} async-done(((f32[8,2,8,128]{3,2,1,0:T(8,128)}), f32[8,2,8,128]{3,2,1,0:T(8,128)S(1)}, u32[]{:S(2)}, u32[]{:S(2)}) %all-to-all-start) | async-done | bytes 65568 | tf_op jit(solution)/shard_map/all_to_all | solution.py:83
  80.2 0.1 fusion.14
  80.3 0.1 divide_convert_fusion
  80.4 13.1 %all-gather = bf16[4,2,2048]{2,1,0:T(2,128)(2,1)S(1)} all-gather(bf16[1,2,2048]{2,1,0:T(2,128)(2,1)S(1)} %bitcast.37), channel_id=1, replica_groups=mesh['group'=2,'lender'=4,'tensor'=4] {'lender'}, dimensions={0}, use_global_device_ids=true | all-gather | bytes 40960 | tf_op jit(solution)/shard_map/all_gather | solution.py:95
  93.6 4.6 %fusion.23 = f32[8,2048]{1,0:T(8,128)S(1)} fusion(bf16[8,2048]{1,0:T(8,128)(2,1)S(1)} %reshape.69, bf16[2048,2048]{1,0:T(8,128)(2,1)} %param.12), kind=kOutput, calls=%fused_computation.44 | convolution fusion | flops 67108864 | bytes 8486912 | tf_op jit(solution)/shard_map/dot_general | solution.py:97
  98.2 10.7 %all-reduce = bf16[8,2048]{1,0:T(8,128)(2,1)S(1)} all-reduce(f32[8,2048]{1,0:T(8,128)S(1)} %fusion.23), channel_id=2, replica_groups=mesh['group'=2,'lender'=4,'tensor'=4] {'tensor'}, use_global_device_ids=true, to_apply=%region_12.13.clone | all-reduce | flops 16384 | bytes 98304
  108.8 0.6 dynamic-slice_convert_fusion
  (18 shorter events, 0.2 us)
Async XLA Ops:
  6.5 44.5 %copy-start = (bf16[2,32,128,128]{3,2,1,0:T(8,128)(2,1)S(1)}, bf16[2,32,128,128]{3,2,1,0:T(8,128)(2,1)}, u32[]{:S(2)}) copy-start(bf16[2,32,128,128]{3,2,1,0:T(8,128)(2,1)} %param.13) | copy-start | bytes 6291460
  6.5 6.2 %copy-start.1 = (bf16[8,2048]{1,0:T(8,128)(2,1)S(1)}, bf16[8,2048]{1,0:T(8,128)(2,1)}, u32[]{:S(2)}) copy-start(bf16[8,2048]{1,0:T(8,128)(2,1)} %param.9) | copy-start | bytes 98308
  6.5 6.3 %copy-start.2 = (s32[8,2,16]{2,1,0:T(2,128)S(1)}, s32[8,2,16]{2,1,0:T(2,128)}, u32[]{:S(2)}) copy-start(s32[8,2,16]{2,1,0:T(2,128)} %param.15) | copy-start | bytes 3076
  6.5 6.4 %copy-start.3 = (s32[2,128]{1,0:T(2,128)S(1)}, s32[2,128]{1,0:T(2,128)}, u32[]{:S(2)}) copy-start(s32[2,128]{1,0:T(2,128)} %param.16) | copy-start | bytes 3076
  6.5 43.4 %all-reduce.3.cloned.1.call-start = ((), (), s32[]{:S(2)}) async-start(), calls=%async_computation.3 | async-start | bytes 131072 | tf_op jit(solution)/shard_map/psum | solution.py:33
  7.4 8.2 %copy-start.4 = (s32[8,2]{0,1:T(2,128)S(1)}, s32[8,2]{0,1:T(2,128)}, u32[]{:S(2)}) copy-start(s32[8,2]{0,1:T(2,128)} %param.17) | copy-start | bytes 196
  7.4 22.1 %copy-start.5 = (u32[32]{0:T(128)S(1)}, u32[32]{0:T(128)}, u32[]{:S(2)}) copy-start(u32[32]{0:T(128)} %constant.64) | copy-start | bytes 388
  53.3 9.0 %all-to-all-start.1 = ((f32[8,2,8]{2,1,0:T(2,128)}), f32[8,2,8]{2,1,0:T(2,128)S(1)}, u32[]{:S(2)}, u32[]{:S(2)}) async-start(f32[8,2,8]{2,1,0:T(2,128)} %copy.57), calls=%async_computation.1 | async-start | bytes 16384 | tf_op jit(solution)/shard_map/all_to_all | solution.py:81
  62.3 8.8 %all-to-all-start.2 = ((f32[8,2,8]{2,1,0:T(2,128)}), f32[8,2,8]{2,1,0:T(2,128)S(1)}, u32[]{:S(2)}, u32[]{:S(2)}) async-start(f32[8,2,8]{2,1,0:T(2,128)} %copy.63), calls=%async_computation.2 | async-start | bytes 16384 | tf_op jit(solution)/shard_map/all_to_all | solution.py:82
  71.1 9.1 %all-to-all-start = ((f32[8,2,8,128]{3,2,1,0:T(8,128)}), f32[8,2,8,128]{3,2,1,0:T(8,128)S(1)}, u32[]{:S(2)}, u32[]{:S(2)}) async-start(f32[8,2,8,128]{3,2,1,0:T(8,128)} %copy.56), calls=%async_computation | async-start | bytes 131072 | tf_op jit(solution)/shard_map/all_to_all | solution.py:83
Sparse Core Ops, SparseCore 0:
  12.8 37.0 all-reduce.2
where the time goes:
time: 117 us; the launch traced here: 116 us
  blocking collectives  37.3 us (32%)
  waiting for transfers between devices  31.5 us (27%)
  between operations  14.2 us (12%)
  matrix products  14 us (12%)
  starting transfers between devices  9.94 us (8%)
  local copies, waits for them, and re-layouts  6.38 us (5%)
  other arithmetic  2.96 us (3%)
    psum x1, waiting for transfers between devices, per_device(): projected, square_sum = lax.psum((partial_value, squares), 'lender')  19.1 us
    psum x1, blocking collectives, per_device(): projected, square_sum = lax.psum((partial_value, squares), 'lender')  13.5 us
    all_gather x1, blocking collectives, per_device(): attended = lax.all_gather(home_attended, 'lender', axis=0, tiled=True)  13.1 us
    unnamed x1, blocking collectives  10.7 us
    all_to_all x1, waiting for transfers between devices, per_device(): lax.all_to_all(row_value, 'lender', split_axis=0, concat_axis=0, tiled=True)  5.54 us
    dot_general x1, matrix products, per_device(): partial_value = jnp.dot(scaled, w_query, preferred_element_type=jnp.float32)  5.24 us
    all_to_all x1, waiting for transfers between devices, per_device(): lax.all_to_all(row_weight, 'lender', split_axis=0, concat_axis=0, tiled=T...  4.68 us
    dot_general x1, matrix products, per_device(): jnp.dot(attended, w_out, preferred_element_type=jnp.float32)  4.57 us
  transfers between devices with their start and end apart: 4, of which 4 were waited for; matrix products, arithmetic and copies ran while one was open for 7% of the time, Pallas kernels for 0%

commit v1 on v0

v1 whole, which is shorter than its diff:
```python
import functools

import jax
import jax.numpy as jnp
from jax import lax
from jax.experimental import pallas as pl
from jax.experimental.pallas import tpu as pltpu
from jax.sharding import PartitionSpec as P

very_low = -1e30
epsilon = 1e-05
LANES = 128
DIRECT_MOST = 8
VMEM = pl.BlockSpec(memory_space=pltpu.VMEM)
HBM = pl.BlockSpec(memory_space=pltpu.HBM)


def project_kernel(
    act_ref, gain_ref, list_ref, table_ref, len_ref, w_ref, out_ref, bias_ref, held, sem, *, chunks
):
    depth, columns = w_ref.shape
    step = depth // chunks
    copies = [
        pltpu.make_async_copy(
            w_ref.at[pl.ds(i * step, step)], held.at[pl.ds(i * step, step)], sem.at[i]
        )
        for i in range(chunks)
    ]
    for copy in copies:
        copy.start()
    rows = act_ref.shape[0]
    features = act_ref[...].astype(jnp.float32)
    squares = jnp.sum(features * features, axis=1, keepdims=True)
    out_ref[:, columns:] = jnp.broadcast_to(squares, (rows, LANES))
    scaled = (features * gain_ref[...].astype(jnp.float32)).astype(jnp.bfloat16)

    kv_heads, blocks = table_ref.shape
    kept_most = list_ref.shape[2]
    slots = bias_ref.shape[1]
    first_slot = lax.axis_index("lender") * slots
    logical = lax.broadcasted_iota(jnp.int32, (rows, blocks), 1)
    own_slot = lax.broadcasted_iota(jnp.int32, (slots, blocks), 0) + first_slot
    for h in range(kv_heads):
        listed = list_ref[:, h, :]
        lens = len_ref[:, h : h + 1]
        kept = jnp.zeros((rows, blocks), jnp.float32)
        for k in range(kept_most):
            entry = jnp.where(lens > k, listed[:, k : k + 1], -1)
            kept = jnp.where(entry == logical, 1.0, kept)
        placed = (own_slot == table_ref[h : h + 1, :]).astype(jnp.bfloat16)
        owned = lax.dot_general(
            kept.astype(jnp.bfloat16),
            placed,
            (((1,), (1,)), ((), ())),
            preferred_element_type=jnp.float32,
        )
        bias = jnp.where(owned > 0.5, 0.0, very_low)
        for s in range(slots):
            bias_ref[h, s] = jnp.broadcast_to(bias[:, s : s + 1], (rows, LANES))

    total = jnp.zeros((rows, columns), jnp.float32)
    for i in range(chunks):
        copies[i].wait()
        total = total + jnp.dot(
            scaled[:, i * step : (i + 1) * step],
            held[i * step : (i + 1) * step, :],
            preferred_element_type=jnp.float32,
        )
    out_ref[:, :columns] = total


def tree_sum(parts):
    while len(parts) > 1:
        parts = [a + b for a, b in zip(parts[::2], parts[1::2])] + parts[len(parts) & ~1 :]
    return parts[0]


def attend_kernel(*refs, parts, width):
    part_refs = refs[:parts]
    bias_ref, key_ref, value_ref, out_ref, score_ref, weight_ref = refs[parts:]
    rows = out_ref.shape[0]
    kv_heads, slots, tokens, head_dim = key_ref.shape
    columns = part_refs[0].shape[1] - LANES
    group = columns // (kv_heads * head_dim)
    heads = kv_heads * group
    square_sum = tree_sum([ref[:, columns:] for ref in part_refs])
    inverse = lax.rsqrt(square_sum / width + epsilon)
    lane = lax.broadcasted_iota(jnp.int32, (rows, LANES), 1)
    all_best = jnp.full((rows, LANES), very_low, jnp.float32)
    all_total = jnp.zeros((rows, LANES), jnp.float32)
    for h in range(kv_heads):
        pieces = []
        for g in range(group):
            at = (h * group + g) * head_dim
            projected = tree_sum([ref[:, at : at + head_dim] for ref in part_refs])
            pieces.append(projected * inverse * head_dim ** (-0.5))
        query = jnp.concatenate(pieces, axis=0).astype(jnp.bfloat16)
        best = jnp.full((group, rows, tokens), very_low, jnp.float32)
        for s in range(slots):
            score = lax.dot_general(
                query,
                key_ref[h, s],
                (((1,), (1,)), ((), ())),
                preferred_element_type=jnp.float32,
            ).reshape(group, rows, tokens)
            score = score + bias_ref[h, s][None]
            best = jnp.maximum(best, score)
            score_ref[:, s * tokens : (s + 1) * tokens] = score.reshape(group * rows, tokens)
        best = jnp.max(best.reshape(group * rows, tokens), axis=1, keepdims=True)
        total = jnp.zeros((group * rows, tokens), jnp.float32)
        for s in range(slots):
            weight = jnp.exp(score_ref[:, s * tokens : (s + 1) * tokens] - best)
            total = total + weight
            weight_ref[:, s * tokens : (s + 1) * tokens] = weight.astype(jnp.bfloat16)
        total = jnp.sum(total, axis=1, keepdims=True)
        summed = jnp.dot(
            weight_ref[...],
            value_ref[h].reshape(slots * tokens, head_dim),
            preferred_element_type=jnp.float32,
        )
        for g in range(group):
            j = h * group + g
            out_ref[:, j * head_dim : (j + 1) * head_dim] = summed[g * rows : (g + 1) * rows]
            all_best = jnp.where(lane == j, best[g * rows : (g + 1) * rows], all_best)
            all_total = jnp.where(lane == j, total[g * rows : (g + 1) * rows], all_total)
    out_ref[:, columns : columns + LANES] = all_best
    out_ref[:, columns + LANES :] = all_total


def output_kernel(*refs, parts, peers, head_dim):
    part_refs = refs[:parts]
    w_ref = refs[parts]
    out_refs = refs[parts + 1 :]
    rows = part_refs[0].shape[0]
    columns = w_ref.shape[0]
    bests = [ref[:, columns : columns + LANES] for ref in part_refs]
    highest = functools.reduce(jnp.maximum, bests)
    factors = [jnp.exp(best - highest) for best in bests]
    total = tree_sum(
        [f * ref[:, columns + LANES :] for f, ref in zip(factors, part_refs)]
    )
    shares = [f / total for f in factors]
    pieces = []
    for j in range(columns // head_dim):
        at = j * head_dim
        pieces.append(
            tree_sum(
                [
                    share[:, j : j + 1] * ref[:, at : at + head_dim]
                    for share, ref in zip(shares, part_refs)
                ]
            )
        )
    attended = jnp.concatenate(pieces, axis=1)
    home = rows // peers
    shift = lax.rem((peers - lax.axis_index("tensor")) * home, rows)
    attended = pltpu.roll(attended, shift, 0).astype(jnp.bfloat16)
    result = jnp.dot(attended, w_ref[...], preferred_element_type=jnp.float32)
    for i, ref in enumerate(out_refs):
        ref[...] = result[i * home : (i + 1) * home]


def send_all(value, axis):
    size = lax.axis_size(axis)
    if size > DIRECT_MOST:
        gathered = lax.all_gather(value, axis)
        return [gathered[i] for i in range(size)]
    if size & (size - 1) == 0:
        tables = [[(i, i ^ s) for i in range(size)] for s in range(1, size)]
    else:
        tables = [[(i, (i + s) % size) for i in range(size)] for s in range(1, size)]
    return [value] + [lax.ppermute(value, axis, table) for table in tables]


def per_device(
    activations,
    norm_gain,
    w_query,
    w_out,
    key_pool,
    value_block_store,
    block_list,
    block_slot_table,
    kept_len,
):
    rows = activations.shape[0]
    depth, columns = w_query.shape
    kv_heads, slots, tokens, head_dim = key_pool.shape
    group = columns // (kv_heads * head_dim)
    lenders = lax.axis_size("lender")
    peers = lax.axis_size("tensor")
    chunks = max(1, min(8, depth // 256))

    payload, bias = pl.pallas_call(
        functools.partial(project_kernel, chunks=chunks),
        out_shape=(
            jax.ShapeDtypeStruct((rows, columns + LANES), jnp.float32),
            jax.ShapeDtypeStruct((kv_heads, slots, rows, LANES), jnp.float32),
        ),
        in_specs=[VMEM] * 5 + [HBM],
        out_specs=(VMEM, VMEM),
        scratch_shapes=[
            pltpu.VMEM((depth, columns), jnp.bfloat16),
            pltpu.SemaphoreType.DMA((chunks,)),
        ],
        compiler_params=pltpu.CompilerParams(vmem_limit_bytes=20 << 20),
        name="project",
    )(
        activations,
        norm_gain[None],
        block_list,
        block_slot_table,
        kept_len,
        pltpu.with_memory_space_constraint(w_query, pltpu.HBM),
    )

    if lenders > DIRECT_MOST:
        parts = [lax.psum(payload, "lender")]
    else:
        parts = send_all(payload, "lender")

    partial_state = pl.pallas_call(
        functools.partial(attend_kernel, parts=len(parts), width=depth * lenders),
        out_shape=jax.ShapeDtypeStruct((rows, columns + 2 * LANES), jnp.float32),
        in_specs=[VMEM] * (len(parts) + 3),
        out_specs=VMEM,
        scratch_shapes=[
            pltpu.VMEM((group * rows, slots * tokens), jnp.float32),
            pltpu.VMEM((group * rows, slots * tokens), jnp.bfloat16),
        ],
        compiler_params=pltpu.CompilerParams(vmem_limit_bytes=24 << 20),
        name="attend",
    )(*parts, bias, key_pool, value_block_store)

    parts = send_all(partial_state, "lender")

    home = rows // peers
    sums = pl.pallas_call(
        functools.partial(output_kernel, parts=len(parts), peers=peers, head_dim=head_dim),
        out_shape=[jax.ShapeDtypeStruct((home, w_out.shape[1]), jnp.float32)] * peers,
        in_specs=[VMEM] * (len(parts) + 1),
        out_specs=[VMEM] * peers,
        compiler_params=pltpu.CompilerParams(vmem_limit_bytes=24 << 20),
        name="output",
    )(*parts, w_out)

    result = sums[0]
    for s in range(1, peers):
        result = result + lax.ppermute(
            sums[s], "tensor", [(i, (i + s) % peers) for i in range(peers)]
        )
    return result.astype(jnp.bfloat16)


def solution(mesh):
    in_specs = (
        P("group", "lender"),
        P("lender"),
        P("lender", "tensor"),
        P("tensor", "lender"),
        P("tensor", ("group", "lender"), None, None),
        P("tensor", ("group", "lender"), None, None),
        P("group", "tensor", None),
        P("tensor", "group"),
        P("group", "tensor"),
    )
    out_specs = P(("group", "tensor"), "lender")
    return jax.shard_map(
        per_device, mesh=mesh, in_specs=in_specs, out_specs=out_specs, check_vma=False
    )
```

time: 117 us -> 39.4 us (0.34)
  blocking collectives: 37.3 us -> 0 us
  waiting for transfers between devices: 31.5 us -> 11.7 us
  between operations: 14.2 us -> 0.04 us
  matrix products: 14 us -> 0 us
  Pallas kernels: 0 us -> 7.51 us
  starting transfers between devices: 9.94 us -> 13.4 us
  other arithmetic: 2.96 us -> 0.62 us
    psum x1 -> x0, waiting for transfers between devices: 19.1 us -> none  [per_device(): projected, square_sum = lax.psum((partial_value, squares), 'lender')]
    dot_general x7 -> x0, matrix products: 14 us -> none  [the longest x1 5.24 us: per_device(): partial_value = jnp.dot(scaled, w_query, preferred_element_type=jnp.float32)]
    psum x1 -> x0, blocking collectives: 13.5 us -> none  [per_device(): projected, square_sum = lax.psum((partial_value, squares), 'lender')]
    ppermute x0 -> x9, starting transfers between devices: none -> 13.4 us  [the longest x6 10.2 us: send_all(): return [value] + [lax.ppermute(value, axis, table) for table in tables]]
    all_gather x1 -> x0, blocking collectives: 13.1 us -> none  [per_device(): attended = lax.all_gather(home_attended, 'lender', axis=0, tiled=True)]
    all_to_all x3 -> x0, waiting for transfers between devices: 12.3 us -> none  [the longest x1 5.54 us: per_device(): lax.all_to_all(row_value, 'lender', split_axis=0, concat_axis=0, tiled=True)]
    ppermute x0 -> x9, waiting for transfers between devices: none -> 11.7 us  [the longest x6 10.3 us: send_all(): return [value] + [lax.ppermute(value, axis, table) for table in tables]]
    unnamed x1 -> x0, blocking collectives: 10.7 us -> none
  transfers between devices with their start and end apart: 4 -> 9, of which waited for: 4 -> 6; matrix products, arithmetic and copies ran while one was open for 7% -> 0% of each run, Pallas kernels for 0% -> 0%
where the time goes in v1:
time: 39.4 us; the launch traced here: 39.2 us
  starting transfers between devices  13.4 us (34%)
  waiting for transfers between devices  11.7 us (30%)
  Pallas kernels  7.51 us (19%)
  local copies, waits for them, and re-layouts  5.91 us (15%)
  other arithmetic  0.62 us (2%)
    ppermute x6, waiting for transfers between devices, send_all(): return [value] + [lax.ppermute(value, axis, table) for table in tables]  10.3 us
    ppermute x6, starting transfers between devices, send_all(): return [value] + [lax.ppermute(value, axis, table) for table in tables]  10.2 us
    unnamed x13, local copies, waits for them, and re-layouts  5.06 us
    pallas_call x1, Pallas kernels, per_device(): pl.pallas_call(functools.partial(project_kernel, chunks=chunks), out_shap...  3.78 us
    ppermute x3, starting transfers between devices, per_device(): lax.ppermute(sums[s], 'tensor', [(i, (i + s) % peers) for i in range(peer...  3.12 us
    pallas_call x1, Pallas kernels, per_device(): pl.pallas_call(functools.partial(attend_kernel, parts=len(parts), width=d...  2.46 us
    ppermute x3, waiting for transfers between devices, per_device(): lax.ppermute(sums[s], 'tensor', [(i, (i + s) % peers) for i in range(peer...  1.44 us
    pallas_call x1, Pallas kernels, per_device(): pl.pallas_call(functools.partial(output_kernel, parts=len(parts), peers=p...  1.27 us
  transfers between devices with their start and end apart: 9, of which 6 were waited for; matrix products, arithmetic and copies ran while one was open for 0% of the time, Pallas kernels for 0%

profile of v1, /device:TPU:0, one launch (start us, length us, event | category | flops | bytes accessed | tf_op | source)
XLA Modules:
  0.0 39.2 jit_solution(1517421694020402030)
XLA Ops:
  0.0 0.0 copy-start.1
  0.0 0.9 %copy.10.len_ref = s32[8,2]{1,0:T(8,128)S(1)} copy(s32[8,2]{0,1:T(2,128)} %param.17) | data formatting | bytes 128 | tf_op args[8]
  0.9 0.0 copy-start
  0.9 0.8 %broadcast_in_dim.3.gain_ref = bf16[1,2048]{1,0:T(2,128)(2,1)S(1)} reshape(bf16[2048]{0:T(1024)(128)(2,1)} %param.10) | data formatting | bytes 8192 | tf_op jit(solution)/shard_map/broadcast_in_dim | solution.py:210
  1.8 0.0 copy-start.3
  1.8 0.9 %copy-done.3 = bf16[8,2048]{1,0:T(8,128)(2,1)S(1)} copy-done((bf16[8,2048]{1,0:T(8,128)(2,1)S(1)}, bf16[8,2048]{1,0:T(8,128)(2,1)}, u32[]{:S(2)}) %copy-start.3) | copy-done | bytes 32792
  2.6 0.0 copy-start.4
  2.6 1.0 %copy-done.4 = s32[8,2,16]{2,1,0:T(2,128)S(1)} copy-done((s32[8,2,16]{2,1,0:T(2,128)S(1)}, s32[8,2,16]{2,1,0:T(2,128)}, u32[]{:S(2)}) %copy-start.4) | copy-done | bytes 1048
  3.6 0.0 copy-start.5
  3.6 0.7 %copy-done.5 = s32[2,128]{1,0:T(2,128)S(1)} copy-done((s32[2,128]{1,0:T(2,128)S(1)}, s32[2,128]{1,0:T(2,128)}, u32[]{:S(2)}) %copy-start.5) | copy-done | bytes 1048
  4.3 3.8 %project.1 = (f32[8,2176]{1,0:T(8,128)S(1)}, f32[2,32,8,128]{3,2,1,0:T(8,128)S(1)}) custom-call(bf16[8,2048]{1,0:T(8,128)(2,1)S(1)} %copy-done.3, bf16[1,2048]{1,0:T(2,128)(2,1)S(1)} %broadcast_in_dim.3.gain_ref, s32[8,2,16]{2,1,0:T(2,128)S(1)} %copy-done.4, s32[2,128]{1,0:T(2,128)S(1)} %copy-done.5, s32[8,2]{1,0:T(8,128)S(1)} %copy.10.len_ref, ...), custom_call_target="tpu_custom_call" | custom-call | tf_op jit(solution)/shard_map/project/pallas_call | solution.py:194
  8.1 5.1 %collective-permute-start.2 = (f32[8,2176]{1,0:T(8,128)S(1)}, f32[8,2176]{1,0:T(8,128)S(1)}, u32[]{:S(2)}, u32[]{:S(2)}) collective-permute-start(f32[8,2176]{1,0:T(8,128)S(1)} %get-tuple-element.11.refs_0_), channel_id=1, source_target_pairs={{0,12},{4,8},{8,4},{12,0},{1,13},{5,9},{9,5},{13,1},{2,14},{6,10},... | collective-permute-start | bytes 208904 | tf_op jit(solution)/shard_map/ppermute | solution.py:172
  13.3 0.0 collective-permute-start.1
  13.3 0.6 %collective-permute-start = (f32[8,2176]{1,0:T(8,128)S(1)}, f32[8,2176]{1,0:T(8,128)S(1)}, u32[]{:S(2)}, u32[]{:S(2)}) collective-permute-start(f32[8,2176]{1,0:T(8,128)S(1)} %get-tuple-element.11.refs_0_), channel_id=1, source_target_pairs={{0,4},{4,0},{8,12},{12,8},{1,5},{5,1},{9,13},{13,9},{2,6},{6,2},{1... | collective-permute-start | bytes 208904 | tf_op jit(solution)/shard_map/ppermute | solution.py:172
  13.9 1.9 %collective-permute-done.2.refs_3_ = f32[8,2176]{1,0:T(8,128)S(1)} collective-permute-done((f32[8,2176]{1,0:T(8,128)S(1)}, f32[8,2176]{1,0:T(8,128)S(1)}, u32[]{:S(2)}, u32[]{:S(2)}) %collective-permute-start.2) | collective-permute-done | bytes 69664 | tf_op jit(solution)/shard_map/ppermute | solution.py:172
  15.8 3.3 %collective-permute-done.1.refs_2_ = f32[8,2176]{1,0:T(8,128)S(1)} collective-permute-done((f32[8,2176]{1,0:T(8,128)S(1)}, f32[8,2176]{1,0:T(8,128)S(1)}, u32[]{:S(2)}, u32[]{:S(2)}) %collective-permute-start.1) | collective-permute-done | bytes 69664 | tf_op jit(solution)/shard_map/ppermute | solution.py:172
  19.2 0.0 collective-permute-done.refs_1_
  19.2 0.0 copy-done.1
  19.2 0.0 copy-start.2
  19.2 1.6 %copy-done.2 = bf16[2,32,128,128]{3,2,1,0:T(8,128)(2,1)S(1)} copy-done((bf16[2,32,128,128]{3,2,1,0:T(8,128)(2,1)S(1)}, bf16[2,32,128,128]{3,2,1,0:T(8,128)(2,1)}, u32[]{:S(2)}) %copy-start.2) | copy-done | bytes 2097176
  20.8 2.5 %attend.1.refs_0_ = f32[8,2304]{1,0:T(8,128)S(1)} custom-call(f32[8,2176]{1,0:T(8,128)S(1)} %get-tuple-element.11.refs_0_, f32[8,2176]{1,0:T(8,128)S(1)} %collective-permute-done.refs_1_, f32[8,2176]{1,0:T(8,128)S(1)} %collective-permute-done.1.refs_2_, f32[8,2176]{1,0:T(8,128)S(1)} %collective-permute-done.2.refs_3_, ...), custom_call_target="tpu_custom_call" | custom-call | tf_op jit(solution)/shard_map/attend/pallas_call | solution.py:222
  23.2 2.8 %collective-permute-start.5 = (f32[8,2304]{1,0:T(8,128)S(1)}, f32[8,2304]{1,0:T(8,128)S(1)}, u32[]{:S(2)}, u32[]{:S(2)}) collective-permute-start(f32[8,2304]{1,0:T(8,128)S(1)} %attend.1.refs_0_), channel_id=1, source_target_pairs={{0,12},{4,8},{8,4},{12,0},{1,13},{5,9},{9,5},{13,1},{2,14},{6,10},... | collective-permute-start | bytes 221192 | tf_op jit(solution)/shard_map/ppermute | solution.py:172
  26.0 0.0 collective-permute-start.4
  26.0 1.7 %collective-permute-start.3 = (f32[8,2304]{1,0:T(8,128)S(1)}, f32[8,2304]{1,0:T(8,128)S(1)}, u32[]{:S(2)}, u32[]{:S(2)}) collective-permute-start(f32[8,2304]{1,0:T(8,128)S(1)} %attend.1.refs_0_), channel_id=1, source_target_pairs={{0,4},{4,0},{8,12},{12,8},{1,5},{5,1},{9,13},{13,9},{2,6},{6,2},{1... | collective-permute-start | bytes 221192 | tf_op jit(solution)/shard_map/ppermute | solution.py:172
  27.7 2.5 %collective-permute-done.5.refs_3_ = f32[8,2304]{1,0:T(8,128)S(1)} collective-permute-done((f32[8,2304]{1,0:T(8,128)S(1)}, f32[8,2304]{1,0:T(8,128)S(1)}, u32[]{:S(2)}, u32[]{:S(2)}) %collective-permute-start.5) | collective-permute-done | bytes 73760 | tf_op jit(solution)/shard_map/ppermute | solution.py:172
  30.2 2.5 %collective-permute-done.4.refs_2_ = f32[8,2304]{1,0:T(8,128)S(1)} collective-permute-done((f32[8,2304]{1,0:T(8,128)S(1)}, f32[8,2304]{1,0:T(8,128)S(1)}, u32[]{:S(2)}, u32[]{:S(2)}) %collective-permute-start.4) | collective-permute-done | bytes 73760 | tf_op jit(solution)/shard_map/ppermute | solution.py:172
  32.7 0.0 collective-permute-done.3.refs_1_
  32.7 0.0 copy-done
  32.7 1.3 %output.1 = (f32[2,2048]{1,0:T(2,128)S(1)}, f32[2,2048]{1,0:T(2,128)S(1)}, f32[2,2048]{1,0:T(2,128)S(1)}, f32[2,2048]{1,0:T(2,128)S(1)}) custom-call(f32[8,2304]{1,0:T(8,128)S(1)} %attend.1.refs_0_, f32[8,2304]{1,0:T(8,128)S(1)} %collective-permute-done.3.refs_1_, f32[8,2304]{1,0:T(8,128)S(1)} %collective-permute-done.4.refs_2_, ...), custom_call_target="tpu_custom_call" | custom-call | tf_op jit(solution)/shard_map/output/pallas_call | solution.py:238
  34.0 0.0 collective-permute-start.6
  34.0 1.7 %collective-permute-start.7 = (f32[2,2048]{1,0:T(2,128)S(1)}, f32[2,2048]{1,0:T(2,128)S(1)}, u32[]{:S(2)}, u32[]{:S(2)}) collective-permute-start(f32[2,2048]{1,0:T(2,128)S(1)} %get-tuple-element.15), channel_id=1, source_target_pairs={{0,2},{1,3},{2,0},{3,1},{4,6},{5,7},{6,4},{7,5},{8,10},{9,11},{10,... | collective-permute-start | bytes 49160 | tf_op jit(solution)/shard_map/ppermute | solution.py:249
  35.7 1.4 %collective-permute-start.8 = (f32[2,2048]{1,0:T(2,128)S(1)}, f32[2,2048]{1,0:T(2,128)S(1)}, u32[]{:S(2)}, u32[]{:S(2)}) collective-permute-start(f32[2,2048]{1,0:T(2,128)S(1)} %get-tuple-element.16), channel_id=1, source_target_pairs={{0,3},{1,0},{2,1},{3,2},{4,7},{5,4},{6,5},{7,6},{8,11},{9,8},{10,9... | collective-permute-start | bytes 49160 | tf_op jit(solution)/shard_map/ppermute | solution.py:249
  37.1 0.0 collective-permute-done.6
  37.2 0.6 %collective-permute-done.7 = f32[2,2048]{1,0:T(2,128)S(1)} collective-permute-done((f32[2,2048]{1,0:T(2,128)S(1)}, f32[2,2048]{1,0:T(2,128)S(1)}, u32[]{:S(2)}, u32[]{:S(2)}) %collective-permute-start.7) | collective-permute-done | bytes 16416 | tf_op jit(solution)/shard_map/ppermute | solution.py:249
  37.8 0.8 %collective-permute-done.8 = f32[2,2048]{1,0:T(2,128)S(1)} collective-permute-done((f32[2,2048]{1,0:T(2,128)S(1)}, f32[2,2048]{1,0:T(2,128)S(1)}, u32[]{:S(2)}, u32[]{:S(2)}) %collective-permute-start.8) | collective-permute-done | bytes 16416 | tf_op jit(solution)/shard_map/ppermute | solution.py:249
  38.5 0.6 %add_convert_fusion = bf16[2,2048]{1,0:T(2,128)(2,1)} fusion(f32[2,2048]{1,0:T(2,128)S(1)} %collective-permute-done.8, f32[2,2048]{1,0:T(2,128)S(1)} %collective-permute-done.7, f32[2,2048]{1,0:T(2,128)S(1)} %get-tuple-element.13, f32[2,2048]{1,0:T(2,128)S(1)} %collective-permute-done.6), kind=kLoop, calls=%fused_computation | loop fusion | flops 16384 | bytes 73728 | tf_op jit(solution)/shard_map/convert_element_type | solution.py:252
Async XLA Ops:
  0.0 19.2 %copy-start.1 = (bf16[2,32,128,128]{3,2,1,0:T(8,128)(2,1)S(1)}, bf16[2,32,128,128]{3,2,1,0:T(8,128)(2,1)}, u32[]{:S(2)}) copy-start(bf16[2,32,128,128]{3,2,1,0:T(8,128)(2,1)} %refs_5_.1) | copy-start | bytes 6291460
  0.9 31.8 %copy-start = (bf16[2048,2048]{1,0:T(8,128)(2,1)S(1)}, bf16[2048,2048]{1,0:T(8,128)(2,1)}, u32[]{:S(2)}) copy-start(bf16[2048,2048]{1,0:T(8,128)(2,1)} %refs_4_.1) | copy-start | bytes 25165828
  1.8 0.9 %copy-start.3 = (bf16[8,2048]{1,0:T(8,128)(2,1)S(1)}, bf16[8,2048]{1,0:T(8,128)(2,1)}, u32[]{:S(2)}) copy-start(bf16[8,2048]{1,0:T(8,128)(2,1)} %act_ref.1) | copy-start | bytes 98308
  2.6 1.0 %copy-start.4 = (s32[8,2,16]{2,1,0:T(2,128)S(1)}, s32[8,2,16]{2,1,0:T(2,128)}, u32[]{:S(2)}) copy-start(s32[8,2,16]{2,1,0:T(2,128)} %list_ref.1) | copy-start | bytes 3076
  3.6 0.7 %copy-start.5 = (s32[2,128]{1,0:T(2,128)S(1)}, s32[2,128]{1,0:T(2,128)}, u32[]{:S(2)}) copy-start(s32[2,128]{1,0:T(2,128)} %table_ref.1) | copy-start | bytes 3076
  8.1 7.7 %collective-permute-start.2 = (f32[8,2176]{1,0:T(8,128)S(1)}, f32[8,2176]{1,0:T(8,128)S(1)}, u32[]{:S(2)}, u32[]{:S(2)}) collective-permute-start(f32[8,2176]{1,0:T(8,128)S(1)} %get-tuple-element.11.refs_0_), channel_id=1, source_target_pairs={{0,12},{4,8},{8,4},{12,0},{1,13},{5,9},{9,5},{13,1},{2,14},{6,10},... | collective-permute-start | bytes 208904 | tf_op jit(solution)/shard_map/ppermute | solution.py:172
  13.3 5.9 %collective-permute-start.1 = (f32[8,2176]{1,0:T(8,128)S(1)}, f32[8,2176]{1,0:T(8,128)S(1)}, u32[]{:S(2)}, u32[]{:S(2)}) collective-permute-start(f32[8,2176]{1,0:T(8,128)S(1)} %get-tuple-element.11.refs_0_), channel_id=1, source_target_pairs={{0,8},{4,12},{8,0},{12,4},{1,9},{5,13},{9,1},{13,5},{2,10},{6,14},... | collective-permute-start | bytes 208904 | tf_op jit(solution)/shard_map/ppermute | solution.py:172
  13.3 5.9 %collective-permute-start = (f32[8,2176]{1,0:T(8,128)S(1)}, f32[8,2176]{1,0:T(8,128)S(1)}, u32[]{:S(2)}, u32[]{:S(2)}) collective-permute-start(f32[8,2176]{1,0:T(8,128)S(1)} %get-tuple-element.11.refs_0_), channel_id=1, source_target_pairs={{0,4},{4,0},{8,12},{12,8},{1,5},{5,1},{9,13},{13,9},{2,6},{6,2},{1... | collective-permute-start | bytes 208904 | tf_op jit(solution)/shard_map/ppermute | solution.py:172
  19.2 1.6 %copy-start.2 = (bf16[2,32,128,128]{3,2,1,0:T(8,128)(2,1)S(1)}, bf16[2,32,128,128]{3,2,1,0:T(8,128)(2,1)}, u32[]{:S(2)}) copy-start(bf16[2,32,128,128]{3,2,1,0:T(8,128)(2,1)} %refs_6_.1) | copy-start | bytes 6291460
  23.2 6.9 %collective-permute-start.5 = (f32[8,2304]{1,0:T(8,128)S(1)}, f32[8,2304]{1,0:T(8,128)S(1)}, u32[]{:S(2)}, u32[]{:S(2)}) collective-permute-start(f32[8,2304]{1,0:T(8,128)S(1)} %attend.1.refs_0_), channel_id=1, source_target_pairs={{0,12},{4,8},{8,4},{12,0},{1,13},{5,9},{9,5},{13,1},{2,14},{6,10},... | collective-permute-start | bytes 221192 | tf_op jit(solution)/shard_map/ppermute | solution.py:172
  26.0 6.7 %collective-permute-start.4 = (f32[8,2304]{1,0:T(8,128)S(1)}, f32[8,2304]{1,0:T(8,128)S(1)}, u32[]{:S(2)}, u32[]{:S(2)}) collective-permute-start(f32[8,2304]{1,0:T(8,128)S(1)} %attend.1.refs_0_), channel_id=1, source_target_pairs={{0,8},{4,12},{8,0},{12,4},{1,9},{5,13},{9,1},{13,5},{2,10},{6,14},... | collective-permute-start | bytes 221192 | tf_op jit(solution)/shard_map/ppermute | solution.py:172
  26.0 6.7 %collective-permute-start.3 = (f32[8,2304]{1,0:T(8,128)S(1)}, f32[8,2304]{1,0:T(8,128)S(1)}, u32[]{:S(2)}, u32[]{:S(2)}) collective-permute-start(f32[8,2304]{1,0:T(8,128)S(1)} %attend.1.refs_0_), channel_id=1, source_target_pairs={{0,4},{4,0},{8,12},{12,8},{1,5},{5,1},{9,13},{13,9},{2,6},{6,2},{1... | collective-permute-start | bytes 221192 | tf_op jit(solution)/shard_map/ppermute | solution.py:172
  34.0 3.2 %collective-permute-start.6 = (f32[2,2048]{1,0:T(2,128)S(1)}, f32[2,2048]{1,0:T(2,128)S(1)}, u32[]{:S(2)}, u32[]{:S(2)}) collective-permute-start(f32[2,2048]{1,0:T(2,128)S(1)} %get-tuple-element.14), channel_id=1, source_target_pairs={{0,1},{1,2},{2,3},{3,0},{4,5},{5,6},{6,7},{7,4},{8,9},{9,10},{10,1... | collective-permute-start | bytes 49160 | tf_op jit(solution)/shard_map/ppermute | solution.py:249
  34.0 3.8 %collective-permute-start.7 = (f32[2,2048]{1,0:T(2,128)S(1)}, f32[2,2048]{1,0:T(2,128)S(1)}, u32[]{:S(2)}, u32[]{:S(2)}) collective-permute-start(f32[2,2048]{1,0:T(2,128)S(1)} %get-tuple-element.15), channel_id=1, source_target_pairs={{0,2},{1,3},{2,0},{3,1},{4,6},{5,7},{6,4},{7,5},{8,10},{9,11},{10,... | collective-permute-start | bytes 49160 | tf_op jit(solution)/shard_map/ppermute | solution.py:249
  35.7 2.9 %collective-permute-start.8 = (f32[2,2048]{1,0:T(2,128)S(1)}, f32[2,2048]{1,0:T(2,128)S(1)}, u32[]{:S(2)}, u32[]{:S(2)}) collective-permute-start(f32[2,2048]{1,0:T(2,128)S(1)} %get-tuple-element.16), channel_id=1, source_target_pairs={{0,3},{1,0},{2,1},{3,2},{4,7},{5,4},{6,5},{7,6},{8,11},{9,8},{10,9... | collective-permute-start | bytes 49160 | tf_op jit(solution)/shard_map/ppermute | solution.py:249

commit v2 on v1

--- a/solution.py
+++ b/solution.py
@@ -16,23 +16,42 @@
 
 
 def project_kernel(
-    act_ref, gain_ref, list_ref, table_ref, len_ref, w_ref, out_ref, bias_ref, held, sem, *, chunks
+    act_hbm, gain_hbm, list_hbm, table_hbm, len_hbm, w_hbm, out_ref, bias_ref,
+    act_ref, gain_ref, list_ref, table_ref, len_ref, held, small_sem, sem, *, chunks
 ):
-    depth, columns = w_ref.shape
+    depth, columns = w_hbm.shape
     step = depth // chunks
+    small = [
+        pltpu.make_async_copy(source, target, small_sem.at[i])
+        for i, (source, target) in enumerate(
+            (
+                (act_hbm, act_ref),
+                (gain_hbm, gain_ref),
+                (list_hbm, list_ref),
+                (table_hbm, table_ref),
+                (len_hbm, len_ref),
+            )
+        )
+    ]
     copies = [
         pltpu.make_async_copy(
-            w_ref.at[pl.ds(i * step, step)], held.at[pl.ds(i * step, step)], sem.at[i]
+            w_hbm.at[pl.ds(i * step, step)], held.at[pl.ds(i * step, step)], sem.at[i]
         )
         for i in range(chunks)
     ]
-    for copy in copies:
+    for copy in small + copies:
         copy.start()
+    for copy in small:
+        copy.wait()
     rows = act_ref.shape[0]
     features = act_ref[...].astype(jnp.float32)
     squares = jnp.sum(features * features, axis=1, keepdims=True)
     out_ref[:, columns:] = jnp.broadcast_to(squares, (rows, LANES))
-    scaled = (features * gain_ref[...].astype(jnp.float32)).astype(jnp.bfloat16)
+    gain = gain_ref[...].astype(jnp.float32)
+    gain = jnp.concatenate(
+        [jnp.broadcast_to(gain[i : i + 1], (rows, LANES)) for i in range(depth // LANES)], axis=1
+    )
+    scaled = (features * gain).astype(jnp.bfloat16)
 
     kv_heads, blocks = table_ref.shape
     kept_most = list_ref.shape[2]
@@ -40,9 +59,12 @@
     first_slot = lax.axis_index("lender") * slots
     logical = lax.broadcasted_iota(jnp.int32, (rows, blocks), 1)
     own_slot = lax.broadcasted_iota(jnp.int32, (slots, blocks), 0) + first_slot
+    diagonal = lax.broadcasted_iota(jnp.int32, (rows, rows), 0) == lax.broadcasted_iota(
+        jnp.int32, (rows, rows), 1
+    )
     for h in range(kv_heads):
         listed = list_ref[:, h, :]
-        lens = len_ref[:, h : h + 1]
+        lens = jnp.sum(jnp.where(diagonal, len_ref[h : h + 1, :], 0), axis=1, keepdims=True)
         kept = jnp.zeros((rows, blocks), jnp.float32)
         for k in range(kept_most):
             entry = jnp.where(lens > k, listed[:, k : k + 1], -1)
@@ -197,21 +219,35 @@
             jax.ShapeDtypeStruct((rows, columns + LANES), jnp.float32),
             jax.ShapeDtypeStruct((kv_heads, slots, rows, LANES), jnp.float32),
         ),
-        in_specs=[VMEM] * 5 + [HBM],
+        in_specs=[HBM] * 6,
         out_specs=(VMEM, VMEM),
         scratch_shapes=[
+            pltpu.VMEM(activations.shape, activations.dtype),
+            pltpu.VMEM((depth // LANES, LANES), norm_gain.dtype),
+            pltpu.VMEM(block_list.shape, block_list.dtype),
+            pltpu.VMEM(block_slot_table.shape, block_slot_table.dtype),
+            pltpu.VMEM(kept_len.shape[::-1], kept_len.dtype),
             pltpu.VMEM((depth, columns), jnp.bfloat16),
+            pltpu.SemaphoreType.DMA((5,)),
             pltpu.SemaphoreType.DMA((chunks,)),
         ],
         compiler_params=pltpu.CompilerParams(vmem_limit_bytes=20 << 20),
         name="project",
     )(
-        activations,
-        norm_gain[None],
-        block_list,
-        block_slot_table,
-        kept_len,
-        pltpu.with_memory_space_constraint(w_query, pltpu.HBM),
+        *(
+            pltpu.with_memory_space_constraint(value, pltpu.HBM)
+            for value in (
+                activations,
+                norm_gain.reshape(-1, LANES),
+                block_list,
+                block_slot_table,
+                kept_len.T,
+                w_query,
+            )
+        )
+    )
+    payload, key_pool, value_block_store, w_out = lax.optimization_barrier(
+        (payload, key_pool, value_block_store, w_out)
     )
 
     if lenders > DIRECT_MOST:

time: 39.4 us -> 34.5 us (0.88)
  local copies, waits for them, and re-layouts: 5.91 us -> 0.01 us
  Pallas kernels: 7.51 us -> 8.64 us
    unnamed x13 -> x6, local copies, waits for them, and re-layouts: 5.06 us -> 0.01 us
    pallas_call x1, Pallas kernels: 3.78 us -> 4.94 us  [per_device(): pl.pallas_call(functools.partial(project_kernel, chunks=chunks), out_shap...]
    broadcast_in_dim x1 -> x0, local copies, waits for them, and re-layouts: 0.84 us -> none  [per_device(): norm_gain[None]]
  transfers between devices with their start and end apart: 9 -> 9, of which waited for: 6 -> 7; matrix products, arithmetic and copies ran while one was open for 0% -> 0% of each run, Pallas kernels for 0% -> 0%
where the time goes in v2:
time: 34.5 us; the launch traced here: 34.4 us
  starting transfers between devices  13.4 us (39%)
  waiting for transfers between devices  11.7 us (34%)
  Pallas kernels  8.64 us (25%)
  other arithmetic  0.62 us (2%)
    ppermute x6, waiting for transfers between devices, send_all(): return [value] + [lax.ppermute(value, axis, table) for table in tables]  10.3 us
    ppermute x6, starting transfers between devices, send_all(): return [value] + [lax.ppermute(value, axis, table) for table in tables]  10.2 us
    pallas_call x1, Pallas kernels, per_device(): pl.pallas_call(functools.partial(project_kernel, chunks=chunks), out_shap...  4.94 us
    ppermute x3, starting transfers between devices, per_device(): lax.ppermute(sums[s], 'tensor', [(i, (i + s) % peers) for i in range(peer...  3.11 us
    pallas_call x1, Pallas kernels, per_device(): pl.pallas_call(functools.partial(attend_kernel, parts=len(parts), width=d...  2.43 us
    ppermute x3, waiting for transfers between devices, per_device(): lax.ppermute(sums[s], 'tensor', [(i, (i + s) % peers) for i in range(peer...  1.44 us
    pallas_call x1, Pallas kernels, per_device(): pl.pallas_call(functools.partial(output_kernel, parts=len(parts), peers=p...  1.27 us
  transfers between devices with their start and end apart: 9, of which 7 were waited for; matrix products, arithmetic and copies ran while one was open for 0% of the time, Pallas kernels for 0%

profile of v2, /device:TPU:0, one launch (start us, length us, event | category | flops | bytes accessed | tf_op | source)
XLA Modules:
  0.0 34.4 jit_solution(12199744641564898429)
XLA Ops:
  0.0 0.0 copy-start.2
  0.0 0.0 copy-start.1
  0.0 0.0 copy-start
  0.0 4.9 %project.1 = (f32[8,2176]{1,0:T(8,128)S(1)}, f32[2,32,8,128]{3,2,1,0:T(8,128)S(1)}) custom-call(bf16[8,2048]{1,0:T(8,128)(2,1)} %act_hbm.1, bf16[16,128]{1,0:T(8,128)(2,1)} %bitcast.2, s32[8,2,16]{2,1,0:T(2,128)} %list_hbm.1, s32[2,128]{1,0:T(2,128)} %table_hbm.1, s32[2,8]{1,0:T(2,128)} %bitcast.3, bf16[2048,2048]{1,0:T(8,128)(2,1)} %w_hbm.1), custom_call_target="tpu_custom_call" | custom-call | tf_op jit(solution)/shard_map/project/pallas_call | solution.py:216
  5.0 5.1 %collective-permute-start.2 = (f32[8,2176]{1,0:T(8,128)S(1)}, f32[8,2176]{1,0:T(8,128)S(1)}, u32[]{:S(2)}, u32[]{:S(2)}) collective-permute-start(f32[8,2176]{1,0:T(8,128)S(1)} %get-tuple-element.16.refs_0_), channel_id=1, source_target_pairs={{0,12},{4,8},{8,4},{12,0},{1,13},{5,9},{9,5},{13,1},{2,14},{6,10},... | collective-permute-start | bytes 208904 | tf_op jit(solution)/shard_map/ppermute | solution.py:194
  10.1 0.0 collective-permute-start.1
  10.1 0.6 %collective-permute-start = (f32[8,2176]{1,0:T(8,128)S(1)}, f32[8,2176]{1,0:T(8,128)S(1)}, u32[]{:S(2)}, u32[]{:S(2)}) collective-permute-start(f32[8,2176]{1,0:T(8,128)S(1)} %get-tuple-element.16.refs_0_), channel_id=1, source_target_pairs={{0,4},{4,0},{8,12},{12,8},{1,5},{5,1},{9,13},{13,9},{2,6},{6,2},{1... | collective-permute-start | bytes 208904 | tf_op jit(solution)/shard_map/ppermute | solution.py:194
  10.7 1.9 %collective-permute-done.2.refs_3_ = f32[8,2176]{1,0:T(8,128)S(1)} collective-permute-done((f32[8,2176]{1,0:T(8,128)S(1)}, f32[8,2176]{1,0:T(8,128)S(1)}, u32[]{:S(2)}, u32[]{:S(2)}) %collective-permute-start.2) | collective-permute-done | bytes 69664 | tf_op jit(solution)/shard_map/ppermute | solution.py:194
  12.7 3.3 %collective-permute-done.1.refs_2_ = f32[8,2176]{1,0:T(8,128)S(1)} collective-permute-done((f32[8,2176]{1,0:T(8,128)S(1)}, f32[8,2176]{1,0:T(8,128)S(1)}, u32[]{:S(2)}, u32[]{:S(2)}) %collective-permute-start.1) | collective-permute-done | bytes 69664 | tf_op jit(solution)/shard_map/ppermute | solution.py:194
  16.0 0.0 collective-permute-done.refs_1_
  16.0 0.0 copy-done.2
  16.0 0.0 copy-done.1
  16.0 2.4 %attend.1.refs_0_ = f32[8,2304]{1,0:T(8,128)S(1)} custom-call(f32[8,2176]{1,0:T(8,128)S(1)} %get-tuple-element.16.refs_0_, f32[8,2176]{1,0:T(8,128)S(1)} %collective-permute-done.refs_1_, f32[8,2176]{1,0:T(8,128)S(1)} %collective-permute-done.1.refs_2_, f32[8,2176]{1,0:T(8,128)S(1)} %collective-permute-done.2.refs_3_, ...), custom_call_target="tpu_custom_call" | custom-call | tf_op jit(solution)/shard_map/attend/pallas_call | solution.py:258
  18.5 2.8 %collective-permute-start.5 = (f32[8,2304]{1,0:T(8,128)S(1)}, f32[8,2304]{1,0:T(8,128)S(1)}, u32[]{:S(2)}, u32[]{:S(2)}) collective-permute-start(f32[8,2304]{1,0:T(8,128)S(1)} %attend.1.refs_0_), channel_id=1, source_target_pairs={{0,12},{4,8},{8,4},{12,0},{1,13},{5,9},{9,5},{13,1},{2,14},{6,10},... | collective-permute-start | bytes 221192 | tf_op jit(solution)/shard_map/ppermute | solution.py:194
  21.3 0.0 collective-permute-start.4
  21.3 1.7 %collective-permute-start.3 = (f32[8,2304]{1,0:T(8,128)S(1)}, f32[8,2304]{1,0:T(8,128)S(1)}, u32[]{:S(2)}, u32[]{:S(2)}) collective-permute-start(f32[8,2304]{1,0:T(8,128)S(1)} %attend.1.refs_0_), channel_id=1, source_target_pairs={{0,4},{4,0},{8,12},{12,8},{1,5},{5,1},{9,13},{13,9},{2,6},{6,2},{1... | collective-permute-start | bytes 221192 | tf_op jit(solution)/shard_map/ppermute | solution.py:194
  22.9 2.5 %collective-permute-done.5.refs_3_ = f32[8,2304]{1,0:T(8,128)S(1)} collective-permute-done((f32[8,2304]{1,0:T(8,128)S(1)}, f32[8,2304]{1,0:T(8,128)S(1)}, u32[]{:S(2)}, u32[]{:S(2)}) %collective-permute-start.5) | collective-permute-done | bytes 73760 | tf_op jit(solution)/shard_map/ppermute | solution.py:194
  25.4 2.5 %collective-permute-done.4.refs_2_ = f32[8,2304]{1,0:T(8,128)S(1)} collective-permute-done((f32[8,2304]{1,0:T(8,128)S(1)}, f32[8,2304]{1,0:T(8,128)S(1)}, u32[]{:S(2)}, u32[]{:S(2)}) %collective-permute-start.4) | collective-permute-done | bytes 73760 | tf_op jit(solution)/shard_map/ppermute | solution.py:194
  27.9 0.0 collective-permute-done.3.refs_1_
  27.9 0.0 copy-done
  28.0 1.3 %output.1 = (f32[2,2048]{1,0:T(2,128)S(1)}, f32[2,2048]{1,0:T(2,128)S(1)}, f32[2,2048]{1,0:T(2,128)S(1)}, f32[2,2048]{1,0:T(2,128)S(1)}) custom-call(f32[8,2304]{1,0:T(8,128)S(1)} %attend.1.refs_0_, f32[8,2304]{1,0:T(8,128)S(1)} %collective-permute-done.3.refs_1_, f32[8,2304]{1,0:T(8,128)S(1)} %collective-permute-done.4.refs_2_, ...), custom_call_target="tpu_custom_call" | custom-call | tf_op jit(solution)/shard_map/output/pallas_call | solution.py:274
  29.2 0.0 collective-permute-start.6
  29.2 1.7 %collective-permute-start.7 = (f32[2,2048]{1,0:T(2,128)S(1)}, f32[2,2048]{1,0:T(2,128)S(1)}, u32[]{:S(2)}, u32[]{:S(2)}) collective-permute-start(f32[2,2048]{1,0:T(2,128)S(1)} %get-tuple-element.23), channel_id=1, source_target_pairs={{0,2},{1,3},{2,0},{3,1},{4,6},{5,7},{6,4},{7,5},{8,10},{9,11},{10,... | collective-permute-start | bytes 49160 | tf_op jit(solution)/shard_map/ppermute | solution.py:285
  30.9 1.4 %collective-permute-start.8 = (f32[2,2048]{1,0:T(2,128)S(1)}, f32[2,2048]{1,0:T(2,128)S(1)}, u32[]{:S(2)}, u32[]{:S(2)}) collective-permute-start(f32[2,2048]{1,0:T(2,128)S(1)} %get-tuple-element.24), channel_id=1, source_target_pairs={{0,3},{1,0},{2,1},{3,2},{4,7},{5,4},{6,5},{7,6},{8,11},{9,8},{10,9... | collective-permute-start | bytes 49160 | tf_op jit(solution)/shard_map/ppermute | solution.py:285
  32.3 0.1 collective-permute-done.6
  32.4 0.6 %collective-permute-done.7 = f32[2,2048]{1,0:T(2,128)S(1)} collective-permute-done((f32[2,2048]{1,0:T(2,128)S(1)}, f32[2,2048]{1,0:T(2,128)S(1)}, u32[]{:S(2)}, u32[]{:S(2)}) %collective-permute-start.7) | collective-permute-done | bytes 16416 | tf_op jit(solution)/shard_map/ppermute | solution.py:285
  33.0 0.8 %collective-permute-done.8 = f32[2,2048]{1,0:T(2,128)S(1)} collective-permute-done((f32[2,2048]{1,0:T(2,128)S(1)}, f32[2,2048]{1,0:T(2,128)S(1)}, u32[]{:S(2)}, u32[]{:S(2)}) %collective-permute-start.8) | collective-permute-done | bytes 16416 | tf_op jit(solution)/shard_map/ppermute | solution.py:285
  33.8 0.6 %add_convert_fusion = bf16[2,2048]{1,0:T(2,128)(2,1)} fusion(f32[2,2048]{1,0:T(2,128)S(1)} %collective-permute-done.8, f32[2,2048]{1,0:T(2,128)S(1)} %collective-permute-done.7, f32[2,2048]{1,0:T(2,128)S(1)} %get-tuple-element.21, f32[2,2048]{1,0:T(2,128)S(1)} %collective-permute-done.6), kind=kLoop, calls=%fused_computation | loop fusion | flops 16384 | bytes 73728 | tf_op jit(solution)/shard_map/convert_element_type | solution.py:288
Async XLA Ops:
  0.0 16.0 %copy-start.2 = (bf16[2,32,128,128]{3,2,1,0:T(8,128)(2,1)S(1)}, bf16[2,32,128,128]{3,2,1,0:T(8,128)(2,1)}, u32[]{:S(2)}) copy-start(bf16[2,32,128,128]{3,2,1,0:T(8,128)(2,1)} %refs_6_) | copy-start | bytes 6291460
  0.0 16.0 %copy-start.1 = (bf16[2,32,128,128]{3,2,1,0:T(8,128)(2,1)S(1)}, bf16[2,32,128,128]{3,2,1,0:T(8,128)(2,1)}, u32[]{:S(2)}) copy-start(bf16[2,32,128,128]{3,2,1,0:T(8,128)(2,1)} %refs_5_) | copy-start | bytes 6291460
  0.0 27.9 %copy-start = (bf16[2048,2048]{1,0:T(8,128)(2,1)S(1)}, bf16[2048,2048]{1,0:T(8,128)(2,1)}, u32[]{:S(2)}) copy-start(bf16[2048,2048]{1,0:T(8,128)(2,1)} %refs_4_) | copy-start | bytes 25165828
  5.0 7.7 %collective-permute-start.2 = (f32[8,2176]{1,0:T(8,128)S(1)}, f32[8,2176]{1,0:T(8,128)S(1)}, u32[]{:S(2)}, u32[]{:S(2)}) collective-permute-start(f32[8,2176]{1,0:T(8,128)S(1)} %get-tuple-element.16.refs_0_), channel_id=1, source_target_pairs={{0,12},{4,8},{8,4},{12,0},{1,13},{5,9},{9,5},{13,1},{2,14},{6,10},... | collective-permute-start | bytes 208904 | tf_op jit(solution)/shard_map/ppermute | solution.py:194
  10.1 5.9 %collective-permute-start.1 = (f32[8,2176]{1,0:T(8,128)S(1)}, f32[8,2176]{1,0:T(8,128)S(1)}, u32[]{:S(2)}, u32[]{:S(2)}) collective-permute-start(f32[8,2176]{1,0:T(8,128)S(1)} %get-tuple-element.16.refs_0_), channel_id=1, source_target_pairs={{0,8},{4,12},{8,0},{12,4},{1,9},{5,13},{9,1},{13,5},{2,10},{6,14},... | collective-permute-start | bytes 208904 | tf_op jit(solution)/shard_map/ppermute | solution.py:194
  10.1 5.9 %collective-permute-start = (f32[8,2176]{1,0:T(8,128)S(1)}, f32[8,2176]{1,0:T(8,128)S(1)}, u32[]{:S(2)}, u32[]{:S(2)}) collective-permute-start(f32[8,2176]{1,0:T(8,128)S(1)} %get-tuple-element.16.refs_0_), channel_id=1, source_target_pairs={{0,4},{4,0},{8,12},{12,8},{1,5},{5,1},{9,13},{13,9},{2,6},{6,2},{1... | collective-permute-start | bytes 208904 | tf_op jit(solution)/shard_map/ppermute | solution.py:194
  18.5 7.0 %collective-permute-start.5 = (f32[8,2304]{1,0:T(8,128)S(1)}, f32[8,2304]{1,0:T(8,128)S(1)}, u32[]{:S(2)}, u32[]{:S(2)}) collective-permute-start(f32[8,2304]{1,0:T(8,128)S(1)} %attend.1.refs_0_), channel_id=1, source_target_pairs={{0,12},{4,8},{8,4},{12,0},{1,13},{5,9},{9,5},{13,1},{2,14},{6,10},... | collective-permute-start | bytes 221192 | tf_op jit(solution)/shard_map/ppermute | solution.py:194
  21.3 6.7 %collective-permute-start.4 = (f32[8,2304]{1,0:T(8,128)S(1)}, f32[8,2304]{1,0:T(8,128)S(1)}, u32[]{:S(2)}, u32[]{:S(2)}) collective-permute-start(f32[8,2304]{1,0:T(8,128)S(1)} %attend.1.refs_0_), channel_id=1, source_target_pairs={{0,8},{4,12},{8,0},{12,4},{1,9},{5,13},{9,1},{13,5},{2,10},{6,14},... | collective-permute-start | bytes 221192 | tf_op jit(solution)/shard_map/ppermute | solution.py:194
  21.3 6.7 %collective-permute-start.3 = (f32[8,2304]{1,0:T(8,128)S(1)}, f32[8,2304]{1,0:T(8,128)S(1)}, u32[]{:S(2)}, u32[]{:S(2)}) collective-permute-start(f32[8,2304]{1,0:T(8,128)S(1)} %attend.1.refs_0_), channel_id=1, source_target_pairs={{0,4},{4,0},{8,12},{12,8},{1,5},{5,1},{9,13},{13,9},{2,6},{6,2},{1... | collective-permute-start | bytes 221192 | tf_op jit(solution)/shard_map/ppermute | solution.py:194
  29.2 3.2 %collective-permute-start.6 = (f32[2,2048]{1,0:T(2,128)S(1)}, f32[2,2048]{1,0:T(2,128)S(1)}, u32[]{:S(2)}, u32[]{:S(2)}) collective-permute-start(f32[2,2048]{1,0:T(2,128)S(1)} %get-tuple-element.22), channel_id=1, source_target_pairs={{0,1},{1,2},{2,3},{3,0},{4,5},{5,6},{6,7},{7,4},{8,9},{9,10},{10,1... | collective-permute-start | bytes 49160 | tf_op jit(solution)/shard_map/ppermute | solution.py:285
  29.2 3.8 %collective-permute-start.7 = (f32[2,2048]{1,0:T(2,128)S(1)}, f32[2,2048]{1,0:T(2,128)S(1)}, u32[]{:S(2)}, u32[]{:S(2)}) collective-permute-start(f32[2,2048]{1,0:T(2,128)S(1)} %get-tuple-element.23), channel_id=1, source_target_pairs={{0,2},{1,3},{2,0},{3,1},{4,6},{5,7},{6,4},{7,5},{8,10},{9,11},{10,... | collective-permute-start | bytes 49160 | tf_op jit(solution)/shard_map/ppermute | solution.py:285
  30.9 2.9 %collective-permute-start.8 = (f32[2,2048]{1,0:T(2,128)S(1)}, f32[2,2048]{1,0:T(2,128)S(1)}, u32[]{:S(2)}, u32[]{:S(2)}) collective-permute-start(f32[2,2048]{1,0:T(2,128)S(1)} %get-tuple-element.24), channel_id=1, source_target_pairs={{0,3},{1,0},{2,1},{3,2},{4,7},{5,4},{6,5},{7,6},{8,11},{9,8},{10,9... | collective-permute-start | bytes 49160 | tf_op jit(solution)/shard_map/ppermute | solution.py:285

commit v3 on v2

v3 whole, which is shorter than its diff:
```python
import functools

import jax
import jax.numpy as jnp
from jax import lax
from jax.experimental import pallas as pl
from jax.experimental.pallas import tpu as pltpu
from jax.sharding import PartitionSpec as P

very_low = -1e30
epsilon = 1e-05
LANES = 128
DIRECT_MOST = 8
VMEM = pl.BlockSpec(memory_space=pltpu.VMEM)
HBM = pl.BlockSpec(memory_space=pltpu.HBM)


def project_kernel(act_hbm, gain_hbm, w_hbm, out_ref, act_ref, gain_ref, held, small_sem, sem):
    depth, columns = w_hbm.shape
    chunks = sem.shape[0]
    step = depth // chunks
    small = [
        pltpu.make_async_copy(act_hbm, act_ref, small_sem.at[0]),
        pltpu.make_async_copy(gain_hbm, gain_ref, small_sem.at[1]),
    ]
    copies = [
        pltpu.make_async_copy(
            w_hbm.at[pl.ds(i * step, step)], held.at[pl.ds(i * step, step)], sem.at[i]
        )
        for i in range(chunks)
    ]
    for copy in small + copies:
        copy.start()
    for copy in small:
        copy.wait()
    rows = act_ref.shape[0]
    features = act_ref[...].astype(jnp.float32)
    squares = jnp.sum(features * features, axis=1, keepdims=True)
    out_ref[:, columns:] = jnp.broadcast_to(squares, (rows, LANES))
    gain = gain_ref[...].astype(jnp.float32)
    gain = jnp.concatenate(
        [jnp.broadcast_to(gain[i : i + 1], (rows, LANES)) for i in range(depth // LANES)], axis=1
    )
    scaled = (features * gain).astype(jnp.bfloat16)
    total = jnp.zeros((rows, columns), jnp.float32)
    for i in range(chunks):
        copies[i].wait()
        total = total + jnp.dot(
            scaled[:, i * step : (i + 1) * step],
            held[i * step : (i + 1) * step, :],
            preferred_element_type=jnp.float32,
        )
    out_ref[:, :columns] = total


def pools_kernel(
    after_hbm, list_hbm, table_hbm, len_hbm, key_hbm, value_hbm, key_ref, value_ref, bias_ref,
    list_ref, table_ref, len_ref, sem
):
    pairs = (
        (list_hbm, list_ref),
        (table_hbm, table_ref),
        (len_hbm, len_ref),
        (key_hbm, key_ref),
        (value_hbm, value_ref),
    )
    copies = [pltpu.make_async_copy(*pair, sem.at[i]) for i, pair in enumerate(pairs)]
    for copy in copies:
        copy.start()
    for copy in copies[:3]:
        copy.wait()
    kv_heads, slots, rows, _ = bias_ref.shape
    blocks = table_ref.shape[1]
    kept_most = list_ref.shape[2]
    first_slot = lax.axis_index("lender") * slots
    logical = lax.broadcasted_iota(jnp.int32, (rows, blocks), 1)
    own_slot = lax.broadcasted_iota(jnp.int32, (slots, blocks), 0) + first_slot
    diagonal = lax.broadcasted_iota(jnp.int32, (rows, rows), 0) == lax.broadcasted_iota(
        jnp.int32, (rows, rows), 1
    )
    for h in range(kv_heads):
        listed = list_ref[:, h, :]
        lens = jnp.sum(jnp.where(diagonal, len_ref[h : h + 1, :], 0), axis=1, keepdims=True)
        kept = jnp.zeros((rows, blocks), jnp.float32)
        for k in range(kept_most):
            entry = jnp.where(lens > k, listed[:, k : k + 1], -1)
            kept = jnp.where(entry == logical, 1.0, kept)
        placed = (own_slot == table_ref[h : h + 1, :]).astype(jnp.bfloat16)
        owned = lax.dot_general(
            kept.astype(jnp.bfloat16),
            placed,
            (((1,), (1,)), ((), ())),
            preferred_element_type=jnp.float32,
        )
        bias = jnp.where(owned > 0.5, 0.0, very_low)
        for s in range(slots):
            bias_ref[h, s] = jnp.broadcast_to(bias[:, s : s + 1], (rows, LANES))
    for copy in copies[3:]:
        copy.wait()


def in_three(value):
    pieces = []
    for _ in range(3):
        piece = value.astype(jnp.bfloat16)
        pieces.append(piece)
        value = value - piece.astype(jnp.float32)
    return pieces


def state_blocks(heads):
    per_tile = max(1, min(6, LANES // heads))
    return [((k % per_tile) * heads, k // per_tile) for k in range(6)], -(-6 // per_tile)


def tree_sum(parts):
    while len(parts) > 1:
        parts = [a + b for a, b in zip(parts[::2], parts[1::2])] + parts[len(parts) & ~1 :]
    return parts[0]


def load_kernel(*refs, count):
    sources, targets, sem = refs[1 : 1 + count], refs[1 + count : 1 + 2 * count], refs[-1]
    copies = [
        pltpu.make_async_copy(source, target, sem.at[i])
        for i, (source, target) in enumerate(zip(sources, targets))
    ]
    for copy in copies:
        copy.start()
    for copy in copies:
        copy.wait()


def in_hbm(*arrays):
    return [pltpu.with_memory_space_constraint(a, pltpu.HBM) for a in arrays]


def load(name, after, *arrays):
    count = len(arrays)
    size = sum(a.size * a.dtype.itemsize for a in arrays)
    return pl.pallas_call(
        functools.partial(load_kernel, count=count),
        out_shape=[jax.ShapeDtypeStruct(a.shape, a.dtype) for a in arrays],
        in_specs=[pl.BlockSpec(memory_space=pl.ANY)] + [HBM] * count,
        out_specs=[VMEM] * count,
        scratch_shapes=[pltpu.SemaphoreType.DMA((count,))],
        compiler_params=pltpu.CompilerParams(vmem_limit_bytes=4 << 20),
        cost_estimate=pl.CostEstimate(flops=0, bytes_accessed=size, transcendentals=0),
        name=name,
    )(after, *in_hbm(*arrays))


def attend_kernel(*refs, parts, width):
    part_refs = refs[:parts]
    bias_ref, key_ref, value_ref, out_ref, score_ref, weight_ref = refs[parts:]
    rows = out_ref.shape[0]
    kv_heads, slots, tokens, head_dim = key_ref.shape
    columns = part_refs[0].shape[1] - LANES
    group = columns // (kv_heads * head_dim)
    heads = kv_heads * group
    both = 2 if kv_heads % 2 == 0 else 1
    lines = group * rows
    some = 2 if slots % 2 == 0 else 1
    square_sum = tree_sum([ref[:, columns:] for ref in part_refs])
    inverse = lax.rsqrt(square_sum / width + epsilon)
    lane = lax.broadcasted_iota(jnp.int32, (rows, LANES), 1)
    places, tiles = state_blocks(heads)
    state = [jnp.zeros((rows, LANES), jnp.float32) for _ in range(tiles)]
    for first in range(0, kv_heads, both):
        pieces = []
        for i in range(both):
            blocks = []
            for g in range(group):
                at = ((first + i) * group + g) * head_dim
                projected = tree_sum([ref[:, at : at + head_dim] for ref in part_refs])
                blocks.append(projected * inverse * head_dim ** (-0.5))
            query = jnp.concatenate(blocks, axis=0).astype(jnp.bfloat16)
            row = [jnp.zeros_like(query)] * both
            row[i] = query
            pieces.append(jnp.concatenate(row, axis=1))
        query = jnp.concatenate(pieces, axis=0)
        best = jnp.full((both, group, rows, tokens), very_low, jnp.float32)
        for s in range(0, slots, some):
            keys = jnp.concatenate(
                [
                    key_ref[first + i, s : s + some].reshape(some * tokens, head_dim)
                    for i in range(both)
                ],
                axis=1,
            )
            score = lax.dot_general(
                query, keys, (((1,), (1,)), ((), ())), preferred_element_type=jnp.float32
            )
            for n in range(some):
                piece = score[:, n * tokens : (n + 1) * tokens]
                piece = piece.reshape(both, group, rows, tokens)
                piece = piece + bias_ref[first : first + both, s + n][:, None]
                best = jnp.maximum(best, piece)
                score_ref[:, (s + n) * tokens : (s + n + 1) * tokens] = piece.reshape(
                    both * lines, tokens
                )
        best = jnp.max(best.reshape(both * lines, tokens), axis=1, keepdims=True)
        total = jnp.zeros((both * lines, tokens), jnp.float32)
        for s in range(slots):
            weight = jnp.exp(score_ref[:, s * tokens : (s + 1) * tokens] - best)
            total = total + weight
            weight_ref[:, s * tokens : (s + 1) * tokens] = weight.astype(jnp.bfloat16)
        total = jnp.sum(total, axis=1, keepdims=True)
        summed = jnp.zeros((both * lines, both * head_dim), jnp.float32)
        for s in range(0, slots, some):
            values = jnp.concatenate(
                [
                    value_ref[first + i, s : s + some].reshape(some * tokens, head_dim)
                    for i in range(both)
                ],
                axis=1,
            )
            summed = summed + jnp.dot(
                weight_ref[:, s * tokens : (s + some) * tokens],
                values,
                preferred_element_type=jnp.float32,
            )
        for i in range(both):
            for g in range(group):
                j = (first + i) * group + g
                at = i * lines + g * rows
                out_ref[:, j * head_dim : (j + 1) * head_dim] = summed[
                    at : at + rows, i * head_dim : (i + 1) * head_dim
                ].astype(out_ref.dtype)
                pieces = in_three(best[at : at + rows]) + in_three(total[at : at + rows])
                for piece, (offset, tile) in zip(pieces, places):
                    state[tile] = jnp.where(
                        lane == offset + j, piece.astype(jnp.float32), state[tile]
                    )
    for tile in range(tiles):
        at = columns + tile * LANES
        out_ref[:, at : at + LANES] = state[tile].astype(out_ref.dtype)


def output_kernel(*refs, parts, peers, head_dim):
    part_refs = refs[:parts]
    w_ref = refs[parts]
    out_refs = refs[parts + 1 :]
    rows = part_refs[0].shape[0]
    columns = w_ref.shape[0]
    heads = columns // head_dim
    places, _ = state_blocks(heads)
    bests, totals = [], []
    for ref in part_refs:
        pieces = []
        for offset, tile in places:
            at = columns + tile * LANES
            block = ref[:, at : at + LANES].astype(jnp.float32)
            pieces.append(pltpu.roll(block, (LANES - offset) % LANES, 1))
        bests.append(pieces[0] + pieces[1] + pieces[2])
        totals.append(pieces[3] + pieces[4] + pieces[5])
    highest = functools.reduce(jnp.maximum, bests)
    factors = [jnp.exp(best - highest) for best in bests]
    total = tree_sum([f * t for f, t in zip(factors, totals)])
    shares = [f / total for f in factors]
    pieces = []
    for j in range(heads):
        at = j * head_dim
        pieces.append(
            tree_sum(
                [
                    share[:, j : j + 1] * ref[:, at : at + head_dim].astype(jnp.float32)
                    for share, ref in zip(shares, part_refs)
                ]
            )
        )
    attended = jnp.concatenate(pieces, axis=1)
    home = rows // peers
    shift = lax.rem((peers - lax.axis_index("tensor")) * home, rows)
    attended = pltpu.roll(attended, shift, 0).astype(jnp.bfloat16)
    result = jnp.dot(attended, w_ref[...], preferred_element_type=jnp.float32)
    for i, ref in enumerate(out_refs):
        ref[...] = result[i * home : (i + 1) * home]


def send_all(value, axis):
    size = lax.axis_size(axis)
    if size > DIRECT_MOST:
        gathered = lax.all_gather(value, axis)
        return [gathered[i] for i in range(size)]
    if size & (size - 1) == 0:
        tables = [[(i, i ^ s) for i in range(size)] for s in range(1, size)]
    else:
        tables = [[(i, (i + s) % size) for i in range(size)] for s in range(1, size)]
    return [value] + [lax.ppermute(value, axis, table) for table in tables]


def per_device(
    activations,
    norm_gain,
    w_query,
    w_out,
    key_pool,
    value_block_store,
    block_list,
    block_slot_table,
    kept_len,
):
    rows = activations.shape[0]
    depth, columns = w_query.shape
    kv_heads, slots, tokens, head_dim = key_pool.shape
    group = columns // (kv_heads * head_dim)
    lenders = lax.axis_size("lender")
    peers = lax.axis_size("tensor")
    both = 2 if kv_heads % 2 == 0 else 1
    chunks = max(1, min(4, depth // 256))

    payload = pl.pallas_call(
        project_kernel,
        out_shape=jax.ShapeDtypeStruct((rows, columns + LANES), jnp.float32),
        in_specs=[HBM] * 3,
        out_specs=VMEM,
        scratch_shapes=[
            pltpu.VMEM(activations.shape, activations.dtype),
            pltpu.VMEM((depth // LANES, LANES), norm_gain.dtype),
            pltpu.VMEM((depth, columns), jnp.bfloat16),
            pltpu.SemaphoreType.DMA((2,)),
            pltpu.SemaphoreType.DMA((chunks,)),
        ],
        compiler_params=pltpu.CompilerParams(vmem_limit_bytes=12 << 20),
        name="project",
    )(*in_hbm(activations, norm_gain.reshape(-1, LANES), w_query))

    key_pool, value_block_store, bias = pl.pallas_call(
        pools_kernel,
        out_shape=(
            jax.ShapeDtypeStruct(key_pool.shape, key_pool.dtype),
            jax.ShapeDtypeStruct(value_block_store.shape, value_block_store.dtype),
            jax.ShapeDtypeStruct((kv_heads, slots, rows, LANES), jnp.float32),
        ),
        in_specs=[pl.BlockSpec(memory_space=pl.ANY)] + [HBM] * 5,
        out_specs=[VMEM] * 3,
        scratch_shapes=[
            pltpu.VMEM(block_list.shape, block_list.dtype),
            pltpu.VMEM(block_slot_table.shape, block_slot_table.dtype),
            pltpu.VMEM(kept_len.shape[::-1], kept_len.dtype),
            pltpu.SemaphoreType.DMA((5,)),
        ],
        compiler_params=pltpu.CompilerParams(vmem_limit_bytes=12 << 20),
        cost_estimate=pl.CostEstimate(
            flops=0, bytes_accessed=4 * key_pool.size, transcendentals=0
        ),
        name="pools",
    )(
        payload,
        *in_hbm(block_list, block_slot_table, kept_len.T, key_pool, value_block_store),
    )

    if lenders > DIRECT_MOST:
        parts = [lax.psum(payload, "lender")]
    else:
        parts = send_all(payload, "lender")

    tiles = state_blocks(kv_heads * group)[1]
    partial_state = pl.pallas_call(
        functools.partial(attend_kernel, parts=len(parts), width=depth * lenders),
        out_shape=jax.ShapeDtypeStruct((rows, columns + tiles * LANES), jnp.bfloat16),
        in_specs=[VMEM] * (len(parts) + 3),
        out_specs=VMEM,
        scratch_shapes=[
            pltpu.VMEM((both * group * rows, slots * tokens), jnp.float32),
            pltpu.VMEM((both * group * rows, slots * tokens), jnp.bfloat16),
        ],
        compiler_params=pltpu.CompilerParams(vmem_limit_bytes=24 << 20),
        name="attend",
    )(*parts, bias, key_pool, value_block_store)

    parts = send_all(partial_state, "lender")
    (w_out,) = load("load_w_out", partial_state, w_out)

    home = rows // peers
    sums = pl.pallas_call(
        functools.partial(output_kernel, parts=len(parts), peers=peers, head_dim=head_dim),
        out_shape=[jax.ShapeDtypeStruct((home, w_out.shape[1]), jnp.float32)] * peers,
        in_specs=[VMEM] * (len(parts) + 1),
        out_specs=[VMEM] * peers,
        compiler_params=pltpu.CompilerParams(vmem_limit_bytes=24 << 20),
        name="output",
    )(*parts, w_out)

    result = sums[0]
    for s in range(1, peers):
        result = result + lax.ppermute(
            sums[s], "tensor", [(i, (i + s) % peers) for i in range(peers)]
        )
    return result.astype(jnp.bfloat16)


def solution(mesh):
    in_specs = (
        P("group", "lender"),
        P("lender"),
        P("lender", "tensor"),
        P("tensor", "lender"),
        P("tensor", ("group", "lender"), None, None),
        P("tensor", ("group", "lender"), None, None),
        P("group", "tensor", None),
        P("tensor", "group"),
        P("group", "tensor"),
    )
    out_specs = P(("group", "tensor"), "lender")
    return jax.shard_map(
        per_device, mesh=mesh, in_specs=in_specs, out_specs=out_specs, check_vma=False
    )
```

time: 34.5 us -> 31.8 us (0.922)
  waiting for transfers between devices: 11.7 us -> 4.39 us
  Pallas kernels: 8.64 us -> 13.2 us
    ppermute x6, waiting for transfers between devices: 10.3 us -> 2.95 us  [send_all(): return [value] + [lax.ppermute(value, axis, table) for table in tables]]
    pallas_call x1 -> x3, Pallas kernels: 4.94 us -> 9.75 us  [the longest x1 4.05 us: per_device(): pl.pallas_call(project_kernel, out_shape=jax.ShapeDtypeStruct((rows, colu...]
  transfers between devices with their start and end apart: 9 -> 9, of which waited for: 7 -> 4; matrix products, arithmetic and copies ran while one was open for 0% -> 0% of each run, Pallas kernels for 0% -> 18%
where the time goes in v3:
time: 31.8 us; the launch traced here: 31.5 us
  Pallas kernels  13.2 us (42%)
  starting transfers between devices  13.2 us (42%)
  waiting for transfers between devices  4.39 us (14%)
  other arithmetic  0.62 us (2%)
    ppermute x6, starting transfers between devices, send_all(): return [value] + [lax.ppermute(value, axis, table) for table in tables]  10.2 us
    pallas_call x1, Pallas kernels, per_device(): pl.pallas_call(project_kernel, out_shape=jax.ShapeDtypeStruct((rows, colu...  4.05 us
    pallas_call x1, Pallas kernels, load(): pl.pallas_call(functools.partial(load_kernel, count=count), out_shape=[ja...  3.39 us
    ppermute x3, starting transfers between devices, per_device(): lax.ppermute(sums[s], 'tensor', [(i, (i + s) % peers) for i in range(peer...  2.96 us
    ppermute x6, waiting for transfers between devices, send_all(): return [value] + [lax.ppermute(value, axis, table) for table in tables]  2.95 us
    pallas_call x1, Pallas kernels, per_device(): pl.pallas_call(pools_kernel, out_shape=(jax.ShapeDtypeStruct(key_pool.sha...  2.31 us
    pallas_call x1, Pallas kernels, per_device(): pl.pallas_call(functools.partial(attend_kernel, parts=len(parts), width=d...  2.1 us
    ppermute x3, waiting for transfers between devices, per_device(): lax.ppermute(sums[s], 'tensor', [(i, (i + s) % peers) for i in range(peer...  1.44 us
  transfers between devices with their start and end apart: 9, of which 4 were waited for; matrix products, arithmetic and copies ran while one was open for 0% of the time, Pallas kernels for 18%

profile of v3, /device:TPU:0, one launch (start us, length us, event | category | flops | bytes accessed | tf_op | source)
XLA Modules:
  0.0 31.5 jit_solution(9179260558641103572)
XLA Ops:
  0.0 4.1 %project.1.after_hbm.refs_0_ = f32[8,2176]{1,0:T(8,128)S(1)} custom-call(bf16[8,2048]{1,0:T(8,128)(2,1)} %act_hbm.1, bf16[16,128]{1,0:T(8,128)(2,1)} %bitcast.2, bf16[2048,2048]{1,0:T(8,128)(2,1)} %w_hbm.1), custom_call_target="tpu_custom_call" | custom-call | tf_op jit(solution)/shard_map/project/pallas_call | solution.py:313
  4.1 5.1 %collective-permute-start.2 = (f32[8,2176]{1,0:T(8,128)S(1)}, f32[8,2176]{1,0:T(8,128)S(1)}, u32[]{:S(2)}, u32[]{:S(2)}) collective-permute-start(f32[8,2176]{1,0:T(8,128)S(1)} %project.1.after_hbm.refs_0_), channel_id=1, source_target_pairs={{0,12},{4,8},{8,4},{12,0},{1,13},{5,9},{9,5},{13,1},{2,14},{6,10},... | collective-permute-start | bytes 208904 | tf_op jit(solution)/shard_map/ppermute | solution.py:290
  9.2 0.0 collective-permute-start.1
  9.2 0.6 %collective-permute-start = (f32[8,2176]{1,0:T(8,128)S(1)}, f32[8,2176]{1,0:T(8,128)S(1)}, u32[]{:S(2)}, u32[]{:S(2)}) collective-permute-start(f32[8,2176]{1,0:T(8,128)S(1)} %project.1.after_hbm.refs_0_), channel_id=1, source_target_pairs={{0,4},{4,0},{8,12},{12,8},{1,5},{5,1},{9,13},{13,9},{2,6},{6,2},{1... | collective-permute-start | bytes 208904 | tf_op jit(solution)/shard_map/ppermute | solution.py:290
  9.8 2.3 %pools.1 = (bf16[2,32,128,128]{3,2,1,0:T(8,128)(2,1)S(1)}, bf16[2,32,128,128]{3,2,1,0:T(8,128)(2,1)S(1)}, f32[2,32,8,128]{3,2,1,0:T(8,128)S(1)}) custom-call(f32[8,2176]{1,0:T(8,128)S(1)} %project.1.after_hbm.refs_0_, s32[8,2,16]{2,1,0:T(2,128)} %list_hbm.1, s32[2,128]{1,0:T(2,128)} %table_hbm.1, s32[2,8]{1,0:T(2,128)} %bitcast.3, ...), custom_call_target="tpu_custom_call" | custom-call | bytes 4194304 | tf_op jit(solution)/shard_map/pools/pallas_call | solution.py:329
  12.2 0.0 collective-permute-done.2.refs_3_
  12.2 2.9 %collective-permute-done.1.refs_2_ = f32[8,2176]{1,0:T(8,128)S(1)} collective-permute-done((f32[8,2176]{1,0:T(8,128)S(1)}, f32[8,2176]{1,0:T(8,128)S(1)}, u32[]{:S(2)}, u32[]{:S(2)}) %collective-permute-start.1) | collective-permute-done | bytes 69664 | tf_op jit(solution)/shard_map/ppermute | solution.py:290
  15.1 0.0 collective-permute-done.refs_1_
  15.1 2.1 %attend.1.refs_0_ = bf16[8,2176]{1,0:T(8,128)(2,1)S(1)} custom-call(f32[8,2176]{1,0:T(8,128)S(1)} %project.1.after_hbm.refs_0_, f32[8,2176]{1,0:T(8,128)S(1)} %collective-permute-done.refs_1_, f32[8,2176]{1,0:T(8,128)S(1)} %collective-permute-done.1.refs_2_, f32[8,2176]{1,0:T(8,128)S(1)} %collective-permute-done.2.refs_3_, ...), custom_call_target="tpu_custom_call" | custom-call | tf_op jit(solution)/shard_map/attend/pallas_call | solution.py:360
  17.2 2.8 %collective-permute-start.5 = (bf16[8,2176]{1,0:T(8,128)(2,1)S(1)}, bf16[8,2176]{1,0:T(8,128)(2,1)S(1)}, u32[]{:S(2)}, u32[]{:S(2)}) collective-permute-start(bf16[8,2176]{1,0:T(8,128)(2,1)S(1)} %attend.1.refs_0_), channel_id=1, source_target_pairs={{0,12},{4,8},{8,4},{12,0},{1,13},{5,9},{9,5},{13,1},{2,14},{6,10},... | collective-permute-start | bytes 104456 | tf_op jit(solution)/shard_map/ppermute | solution.py:290
  20.0 0.0 collective-permute-start.4
  20.0 1.7 %collective-permute-start.3 = (bf16[8,2176]{1,0:T(8,128)(2,1)S(1)}, bf16[8,2176]{1,0:T(8,128)(2,1)S(1)}, u32[]{:S(2)}, u32[]{:S(2)}) collective-permute-start(bf16[8,2176]{1,0:T(8,128)(2,1)S(1)} %attend.1.refs_0_), channel_id=1, source_target_pairs={{0,4},{4,0},{8,12},{12,8},{1,5},{5,1},{9,13},{13,9},{2,6},{6,2},{1... | collective-permute-start | bytes 104456 | tf_op jit(solution)/shard_map/ppermute | solution.py:290
  21.7 3.4 %load_w_out.1.refs_4_ = bf16[2048,2048]{1,0:T(8,128)(2,1)S(1)} custom-call(bf16[8,2176]{1,0:T(8,128)(2,1)S(1)} %attend.1.refs_0_, bf16[2048,2048]{1,0:T(8,128)(2,1)} %refs_1_.1), custom_call_target="tpu_custom_call" | custom-call | bytes 8388608 | tf_op jit(solution)/shard_map/load_w_out/pallas_call | solution.py:141
  25.1 0.0 collective-permute-done.5.refs_3_
  25.1 0.0 collective-permute-done.4.refs_2_
  25.1 0.0 collective-permute-done.3.refs_1_
  25.1 1.3 %output.1 = (f32[2,2048]{1,0:T(2,128)S(1)}, f32[2,2048]{1,0:T(2,128)S(1)}, f32[2,2048]{1,0:T(2,128)S(1)}, f32[2,2048]{1,0:T(2,128)S(1)}) custom-call(bf16[8,2176]{1,0:T(8,128)(2,1)S(1)} %attend.1.refs_0_, bf16[8,2176]{1,0:T(8,128)(2,1)S(1)} %collective-permute-done.3.refs_1_, bf16[8,2176]{1,0:T(8,128)(2,1)S(1)} %collective-permute-done.4.refs_2_, ...), custom_call_target="tpu_custom_call" | custom-call | tf_op jit(solution)/shard_map/output/pallas_call | solution.py:377
  26.5 0.0 collective-permute-start.6
  26.5 1.5 %collective-permute-start.7 = (f32[2,2048]{1,0:T(2,128)S(1)}, f32[2,2048]{1,0:T(2,128)S(1)}, u32[]{:S(2)}, u32[]{:S(2)}) collective-permute-start(f32[2,2048]{1,0:T(2,128)S(1)} %get-tuple-element.17), channel_id=1, source_target_pairs={{0,2},{1,3},{2,0},{3,1},{4,6},{5,7},{6,4},{7,5},{8,10},{9,11},{10,... | collective-permute-start | bytes 49160 | tf_op jit(solution)/shard_map/ppermute | solution.py:388
  28.0 1.4 %collective-permute-start.8 = (f32[2,2048]{1,0:T(2,128)S(1)}, f32[2,2048]{1,0:T(2,128)S(1)}, u32[]{:S(2)}, u32[]{:S(2)}) collective-permute-start(f32[2,2048]{1,0:T(2,128)S(1)} %get-tuple-element.18), channel_id=1, source_target_pairs={{0,3},{1,0},{2,1},{3,2},{4,7},{5,4},{6,5},{7,6},{8,11},{9,8},{10,9... | collective-permute-start | bytes 49160 | tf_op jit(solution)/shard_map/ppermute | solution.py:388
  29.4 0.2 collective-permute-done.6
  29.6 0.6 %collective-permute-done.7 = f32[2,2048]{1,0:T(2,128)S(1)} collective-permute-done((f32[2,2048]{1,0:T(2,128)S(1)}, f32[2,2048]{1,0:T(2,128)S(1)}, u32[]{:S(2)}, u32[]{:S(2)}) %collective-permute-start.7) | collective-permute-done | bytes 16416 | tf_op jit(solution)/shard_map/ppermute | solution.py:388
  30.2 0.6 %collective-permute-done.8 = f32[2,2048]{1,0:T(2,128)S(1)} collective-permute-done((f32[2,2048]{1,0:T(2,128)S(1)}, f32[2,2048]{1,0:T(2,128)S(1)}, u32[]{:S(2)}, u32[]{:S(2)}) %collective-permute-start.8) | collective-permute-done | bytes 16416 | tf_op jit(solution)/shard_map/ppermute | solution.py:388
  30.9 0.6 %add_convert_fusion = bf16[2,2048]{1,0:T(2,128)(2,1)} fusion(f32[2,2048]{1,0:T(2,128)S(1)} %collective-permute-done.8, f32[2,2048]{1,0:T(2,128)S(1)} %collective-permute-done.7, f32[2,2048]{1,0:T(2,128)S(1)} %get-tuple-element.15, f32[2,2048]{1,0:T(2,128)S(1)} %collective-permute-done.6), kind=kLoop, calls=%fused_computation | loop fusion | flops 16384 | bytes 73728 | tf_op jit(solution)/shard_map/convert_element_type | solution.py:391
Async XLA Ops:
  4.1 8.1 %collective-permute-start.2 = (f32[8,2176]{1,0:T(8,128)S(1)}, f32[8,2176]{1,0:T(8,128)S(1)}, u32[]{:S(2)}, u32[]{:S(2)}) collective-permute-start(f32[8,2176]{1,0:T(8,128)S(1)} %project.1.after_hbm.refs_0_), channel_id=1, source_target_pairs={{0,12},{4,8},{8,4},{12,0},{1,13},{5,9},{9,5},{13,1},{2,14},{6,10},... | collective-permute-start | bytes 208904 | tf_op jit(solution)/shard_map/ppermute | solution.py:290
  9.2 5.9 %collective-permute-start.1 = (f32[8,2176]{1,0:T(8,128)S(1)}, f32[8,2176]{1,0:T(8,128)S(1)}, u32[]{:S(2)}, u32[]{:S(2)}) collective-permute-start(f32[8,2176]{1,0:T(8,128)S(1)} %project.1.after_hbm.refs_0_), channel_id=1, source_target_pairs={{0,8},{4,12},{8,0},{12,4},{1,9},{5,13},{9,1},{13,5},{2,10},{6,14},... | collective-permute-start | bytes 208904 | tf_op jit(solution)/shard_map/ppermute | solution.py:290
  9.2 5.9 %collective-permute-start = (f32[8,2176]{1,0:T(8,128)S(1)}, f32[8,2176]{1,0:T(8,128)S(1)}, u32[]{:S(2)}, u32[]{:S(2)}) collective-permute-start(f32[8,2176]{1,0:T(8,128)S(1)} %project.1.after_hbm.refs_0_), channel_id=1, source_target_pairs={{0,4},{4,0},{8,12},{12,8},{1,5},{5,1},{9,13},{13,9},{2,6},{6,2},{1... | collective-permute-start | bytes 208904 | tf_op jit(solution)/shard_map/ppermute | solution.py:290
  17.2 7.9 %collective-permute-start.5 = (bf16[8,2176]{1,0:T(8,128)(2,1)S(1)}, bf16[8,2176]{1,0:T(8,128)(2,1)S(1)}, u32[]{:S(2)}, u32[]{:S(2)}) collective-permute-start(bf16[8,2176]{1,0:T(8,128)(2,1)S(1)} %attend.1.refs_0_), channel_id=1, source_target_pairs={{0,12},{4,8},{8,4},{12,0},{1,13},{5,9},{9,5},{13,1},{2,14},{6,10},... | collective-permute-start | bytes 104456 | tf_op jit(solution)/shard_map/ppermute | solution.py:290
  20.0 5.1 %collective-permute-start.4 = (bf16[8,2176]{1,0:T(8,128)(2,1)S(1)}, bf16[8,2176]{1,0:T(8,128)(2,1)S(1)}, u32[]{:S(2)}, u32[]{:S(2)}) collective-permute-start(bf16[8,2176]{1,0:T(8,128)(2,1)S(1)} %attend.1.refs_0_), channel_id=1, source_target_pairs={{0,8},{4,12},{8,0},{12,4},{1,9},{5,13},{9,1},{13,5},{2,10},{6,14},... | collective-permute-start | bytes 104456 | tf_op jit(solution)/shard_map/ppermute | solution.py:290
  20.0 5.1 %collective-permute-start.3 = (bf16[8,2176]{1,0:T(8,128)(2,1)S(1)}, bf16[8,2176]{1,0:T(8,128)(2,1)S(1)}, u32[]{:S(2)}, u32[]{:S(2)}) collective-permute-start(bf16[8,2176]{1,0:T(8,128)(2,1)S(1)} %attend.1.refs_0_), channel_id=1, source_target_pairs={{0,4},{4,0},{8,12},{12,8},{1,5},{5,1},{9,13},{13,9},{2,6},{6,2},{1... | collective-permute-start | bytes 104456 | tf_op jit(solution)/shard_map/ppermute | solution.py:290
  26.5 3.2 %collective-permute-start.6 = (f32[2,2048]{1,0:T(2,128)S(1)}, f32[2,2048]{1,0:T(2,128)S(1)}, u32[]{:S(2)}, u32[]{:S(2)}) collective-permute-start(f32[2,2048]{1,0:T(2,128)S(1)} %get-tuple-element.16), channel_id=1, source_target_pairs={{0,1},{1,2},{2,3},{3,0},{4,5},{5,6},{6,7},{7,4},{8,9},{9,10},{10,1... | collective-permute-start | bytes 49160 | tf_op jit(solution)/shard_map/ppermute | solution.py:388
  26.5 3.8 %collective-permute-start.7 = (f32[2,2048]{1,0:T(2,128)S(1)}, f32[2,2048]{1,0:T(2,128)S(1)}, u32[]{:S(2)}, u32[]{:S(2)}) collective-permute-start(f32[2,2048]{1,0:T(2,128)S(1)} %get-tuple-element.17), channel_id=1, source_target_pairs={{0,2},{1,3},{2,0},{3,1},{4,6},{5,7},{6,4},{7,5},{8,10},{9,11},{10,... | collective-permute-start | bytes 49160 | tf_op jit(solution)/shard_map/ppermute | solution.py:388
  28.0 2.9 %collective-permute-start.8 = (f32[2,2048]{1,0:T(2,128)S(1)}, f32[2,2048]{1,0:T(2,128)S(1)}, u32[]{:S(2)}, u32[]{:S(2)}) collective-permute-start(f32[2,2048]{1,0:T(2,128)S(1)} %get-tuple-element.18), channel_id=1, source_target_pairs={{0,3},{1,0},{2,1},{3,2},{4,7},{5,4},{6,5},{7,6},{8,11},{9,8},{10,9... | collective-permute-start | bytes 49160 | tf_op jit(solution)/shard_map/ppermute | solution.py:388

commit v4 on v3

v4 whole, which is shorter than its diff:
```python
import functools

import jax
import jax.numpy as jnp
from jax import lax
from jax.experimental import pallas as pl
from jax.experimental.pallas import tpu as pltpu
from jax.sharding import PartitionSpec as P

very_low = -1e30
epsilon = 1e-05
LANES = 128
DIRECT_MOST = 8
VMEM = pl.BlockSpec(memory_space=pltpu.VMEM)
HBM = pl.BlockSpec(memory_space=pltpu.HBM)


def in_three(value):
    pieces = []
    for _ in range(3):
        piece = value.astype(jnp.bfloat16)
        pieces.append(piece)
        value = value - piece.astype(jnp.float32)
    return pieces


def project_kernel(
    act_hbm, gain_hbm, w_hbm, out_ref, act_ref, gain_ref, held, small_sem, sem
):
    depth, columns = w_hbm.shape
    chunks = sem.shape[0]
    step = depth // chunks
    small = [
        pltpu.make_async_copy(act_hbm, act_ref, small_sem.at[0]),
        pltpu.make_async_copy(gain_hbm, gain_ref, small_sem.at[1]),
    ]
    copies = [
        pltpu.make_async_copy(
            w_hbm.at[pl.ds(i * step, step)], held.at[pl.ds(i * step, step)], sem.at[i]
        )
        for i in range(chunks)
    ]
    for copy in small + copies:
        copy.start()
    for copy in small:
        copy.wait()
    rows = act_ref.shape[0]
    features = act_ref[...].astype(jnp.float32)
    squares = jnp.sum(features * features, axis=1, keepdims=True)
    out_ref[:, columns:] = jnp.broadcast_to(squares, (rows, LANES))
    gain = gain_ref[...].astype(jnp.float32)
    gain = jnp.concatenate(
        [jnp.broadcast_to(gain[i : i + 1], (rows, LANES)) for i in range(depth // LANES)], axis=1
    )
    scaled = (features * gain).astype(jnp.bfloat16)
    total = jnp.zeros((rows, columns), jnp.float32)
    for i in range(chunks):
        copies[i].wait()
        total = total + jnp.dot(
            scaled[:, i * step : (i + 1) * step],
            held[i * step : (i + 1) * step, :],
            preferred_element_type=jnp.float32,
        )
    out_ref[:, :columns] = total


def owners_kernel(
    after_hbm, list_hbm, table_hbm, len_hbm, pick_ref, gather_ref, bias_ref,
    list_ref, table_ref, len_ref, sem
):
    pairs = ((list_hbm, list_ref), (table_hbm, table_ref), (len_hbm, len_ref))
    copies = [pltpu.make_async_copy(*pair, sem.at[i]) for i, pair in enumerate(pairs)]
    for copy in copies:
        copy.start()
    for copy in copies:
        copy.wait()
    kv_heads, spots, lines = pick_ref.shape
    rows, _, kept_most = list_ref.shape
    blocks = table_ref.shape[1]
    group = lines // rows
    first_slot = lax.axis_index("lender") * (spots // group)
    logical = lax.broadcasted_iota(jnp.int32, (rows, blocks), 1)
    own_slot = lax.broadcasted_iota(jnp.int32, (spots, blocks), 0) // group + first_slot
    diagonal = lax.broadcasted_iota(jnp.int32, (rows, rows), 0) == lax.broadcasted_iota(
        jnp.int32, (rows, rows), 1
    )
    pick_mask = lax.rem(lax.broadcasted_iota(jnp.int32, (spots, lines), 0), group) == (
        lax.broadcasted_iota(jnp.int32, (spots, lines), 1) // rows
    )
    gather_mask = lax.rem(lax.broadcasted_iota(jnp.int32, (lines, spots), 1), group) == (
        lax.broadcasted_iota(jnp.int32, (lines, spots), 0) // rows
    )
    for h in range(kv_heads):
        listed = list_ref[:, h, :]
        lens = jnp.sum(jnp.where(diagonal, len_ref[h : h + 1, :], 0), axis=1, keepdims=True)
        kept = jnp.zeros((rows, blocks), jnp.float32)
        for k in range(kept_most):
            entry = jnp.where(lens > k, listed[:, k : k + 1], -1)
            kept = jnp.where(entry == logical, 1.0, kept)
        kept = jnp.concatenate([kept] * group, axis=0).astype(jnp.bfloat16)
        placed = jnp.where(own_slot == table_ref[h : h + 1, :], 1.0, 0.0).astype(jnp.bfloat16)
        last = (((1,), (1,)), ((), ()))
        owned = lax.dot_general(placed, kept, last, preferred_element_type=jnp.float32)
        owned = jnp.where(pick_mask, owned, 0.0)
        pick_ref[h] = owned.astype(jnp.bfloat16)
        bias_ref[h] = jnp.where(owned > 0.5, 0.0, very_low)
        owned = lax.dot_general(kept, placed, last, preferred_element_type=jnp.float32)
        gather_ref[h] = jnp.where(gather_mask, owned, 0.0).astype(jnp.bfloat16)


def state_blocks(heads):
    per_tile = max(1, min(6, LANES // heads))
    return [((k % per_tile) * heads, k // per_tile) for k in range(6)], -(-6 // per_tile)


def tree_sum(parts):
    while len(parts) > 1:
        parts = [a + b for a, b in zip(parts[::2], parts[1::2])] + parts[len(parts) & ~1 :]
    return parts[0]


def in_hbm(*arrays):
    return [pltpu.with_memory_space_constraint(a, pltpu.HBM) for a in arrays]


def attend_kernel(*refs, parts, width):
    part_refs = refs[:parts]
    pick_ref, gather_ref, bias_ref, key_ref, value_ref, out_ref = refs[parts:]
    rows = out_ref.shape[0]
    kv_heads, slots, tokens, head_dim = key_ref.shape
    columns = part_refs[0].shape[1] - LANES
    group = columns // (kv_heads * head_dim)
    heads = kv_heads * group
    lines = group * rows
    both = 2 if kv_heads % 2 == 0 else 1
    some = 2 if slots % 2 == 0 else 1
    square_sum = tree_sum([ref[:, columns:] for ref in part_refs])
    inverse = lax.rsqrt(square_sum / width + epsilon)
    lane = lax.broadcasted_iota(jnp.int32, (rows, LANES), 1)
    line = lax.broadcasted_iota(jnp.int32, (rows, lines), 1)
    row = lax.broadcasted_iota(jnp.int32, (rows, lines), 0)
    all_best = jnp.zeros((rows, LANES), jnp.float32)
    all_total = jnp.zeros((rows, LANES), jnp.float32)
    for first in range(0, kv_heads, both):
        chosen = []
        for i in range(both):
            blocks = []
            for g in range(group):
                at = ((first + i) * group + g) * head_dim
                projected = tree_sum([ref[:, at : at + head_dim] for ref in part_refs])
                blocks.append(projected * inverse * head_dim ** (-0.5))
            query = jnp.concatenate(blocks, axis=0).astype(jnp.bfloat16)
            chosen.append(
                jnp.dot(pick_ref[first + i], query, preferred_element_type=jnp.float32)
            )
        bests = [[] for _ in range(both)]
        totals = [[] for _ in range(both)]
        values = [[] for _ in range(both)]

        def spread(pieces, at, count):
            zero = jnp.zeros_like(pieces[0])
            lined = [
                jnp.concatenate([p if c == where else zero for c in range(count)], axis=1)
                for p, where in zip(pieces, at)
            ]
            return jnp.concatenate(lined, axis=0).astype(jnp.bfloat16)

        def stacked(ref, s):
            return jnp.concatenate(
                [ref[first + i, s : s + some].reshape(some * tokens, head_dim) for i in range(both)],
                axis=1,
            )

        pairs = [(n, i) for n in range(some) for i in range(both)]
        scores, weights = [], []
        for s in range(0, slots, some):
            query = spread(
                [chosen[i][(s + n) * group : (s + n + 1) * group] for n, i in pairs],
                [i for _, i in pairs],
                both,
            )
            score = lax.dot_general(
                query,
                stacked(key_ref, s),
                (((1,), (1,)), ((), ())),
                preferred_element_type=jnp.float32,
            )
            scores += [
                score[at * group : (at + 1) * group, n * tokens : (n + 1) * tokens]
                for at, (n, i) in enumerate(pairs)
            ]
        for at, score in enumerate(scores):
            best = jnp.max(score, axis=1, keepdims=True)
            weight = jnp.exp(score - best)
            i = pairs[at % len(pairs)][1]
            bests[i].append(best)
            totals[i].append(jnp.sum(weight, axis=1, keepdims=True))
            weights.append(weight)
        for s in range(0, slots, some):
            at = s // some * len(pairs)
            summed = jnp.dot(
                spread(weights[at : at + len(pairs)], [n for n, _ in pairs], some),
                stacked(value_ref, s),
                preferred_element_type=jnp.float32,
            )
            for at, (n, i) in enumerate(pairs):
                values[i].append(
                    summed[at * group : (at + 1) * group, i * head_dim : (i + 1) * head_dim]
                )
        for i in range(both):
            h = first + i
            marked = [
                bias_ref[h, s * group : (s + 1) * group, :] + best
                for s, best in enumerate(bests[i])
            ]
            highest = jnp.max(functools.reduce(jnp.maximum, marked), axis=0, keepdims=True)
            against = jnp.maximum(highest, 0.5 * very_low)
            factors = [jnp.exp(m - against) for m in marked]
            total = jnp.sum(
                tree_sum([f * t for f, t in zip(factors, totals[i])]), axis=0, keepdims=True
            )
            scaled = jnp.concatenate(
                [
                    jnp.sum(f, axis=1, keepdims=True) * v
                    for f, v in zip(factors, values[i])
                ],
                axis=0,
            )
            high = scaled.astype(jnp.bfloat16)
            low = (scaled - high.astype(jnp.float32)).astype(jnp.bfloat16)
            summed = jnp.dot(
                gather_ref[h],
                jnp.concatenate([high, low], axis=1),
                preferred_element_type=jnp.float32,
            )
            summed = summed[:, :head_dim] + summed[:, head_dim:]
            for g in range(group):
                j = h * group + g
                out_ref[:, j * head_dim : (j + 1) * head_dim] = summed[
                    g * rows : (g + 1) * rows
                ].astype(out_ref.dtype)
                here = line == g * rows + row
                best = jnp.sum(jnp.where(here, highest, 0.0), axis=1, keepdims=True)
                sums = jnp.sum(jnp.where(here, total, 0.0), axis=1, keepdims=True)
                all_best = jnp.where(lane == j, best, all_best)
                all_total = jnp.where(lane == j, sums, all_total)
    places, tiles = state_blocks(heads)
    state = [jnp.zeros((rows, LANES), jnp.float32) for _ in range(tiles)]
    for piece, (offset, tile) in zip(in_three(all_best) + in_three(all_total), places):
        state[tile] = state[tile] + pltpu.roll(piece.astype(jnp.float32), offset, 1)
    for tile in range(tiles):
        at = columns + tile * LANES
        out_ref[:, at : at + LANES] = state[tile].astype(out_ref.dtype)


def swap_homes(value, home, peers):
    row = lax.broadcasted_iota(jnp.int32, value.shape, 0)
    mine = lax.axis_index("tensor")
    step = home
    while step < home * peers:
        size = value.shape[0]
        lower = lax.rem(row // step, 2) == 0
        other = jnp.where(
            lower, pltpu.roll(value, size - step, 0), pltpu.roll(value, step, 0)
        )
        value = jnp.where(lax.rem(mine // (step // home), 2) == 1, other, value)
        step *= 2
    return value


def output_kernel(*refs, parts, peers, head_dim):
    part_refs = refs[:parts]
    w_ref = refs[parts]
    out_refs = refs[parts + 1 :]
    rows = part_refs[0].shape[0]
    columns = w_ref.shape[0]
    heads = columns // head_dim
    places, _ = state_blocks(heads)
    bests, totals = [], []
    for ref in part_refs:
        pieces = []
        for offset, tile in places:
            at = columns + tile * LANES
            block = ref[:, at : at + LANES].astype(jnp.float32)
            pieces.append(pltpu.roll(block, (LANES - offset) % LANES, 1))
        bests.append(pieces[0] + pieces[1] + pieces[2])
        totals.append(pieces[3] + pieces[4] + pieces[5])
    highest = functools.reduce(jnp.maximum, bests)
    factors = [jnp.exp(best - highest) for best in bests]
    total = tree_sum([f * t for f, t in zip(factors, totals)])
    shares = [f / total for f in factors]
    pieces = []
    for j in range(heads):
        at = j * head_dim
        pieces.append(
            tree_sum(
                [
                    share[:, j : j + 1] * ref[:, at : at + head_dim].astype(jnp.float32)
                    for share, ref in zip(shares, part_refs)
                ]
            )
        )
    attended = jnp.concatenate(pieces, axis=1)
    home = rows // peers
    attended = swap_homes(attended, home, peers).astype(jnp.bfloat16)
    result = jnp.dot(attended, w_ref[...], preferred_element_type=jnp.float32)
    for i, ref in enumerate(out_refs):
        ref[...] = result[i * home : (i + 1) * home]


def send_all(value, axis):
    size = lax.axis_size(axis)
    if size > DIRECT_MOST:
        gathered = lax.all_gather(value, axis)
        return [gathered[i] for i in range(size)]
    if size & (size - 1) == 0:
        tables = [[(i, i ^ s) for i in range(size)] for s in range(1, size)]
    else:
        tables = [[(i, (i + s) % size) for i in range(size)] for s in range(1, size)]
    return [value] + [lax.ppermute(value, axis, table) for table in tables]


def per_device(
    activations,
    norm_gain,
    w_query,
    w_out,
    key_pool,
    value_block_store,
    block_list,
    block_slot_table,
    kept_len,
):
    rows = activations.shape[0]
    depth, columns = w_query.shape
    kv_heads, slots, tokens, head_dim = key_pool.shape
    group = columns // (kv_heads * head_dim)
    lenders = lax.axis_size("lender")
    peers = lax.axis_size("tensor")
    chunks = max(1, min(4, depth // 256))

    payload = pl.pallas_call(
        project_kernel,
        out_shape=jax.ShapeDtypeStruct((rows, columns + LANES), jnp.float32),
        in_specs=[HBM] * 3,
        out_specs=VMEM,
        scratch_shapes=[
            pltpu.VMEM(activations.shape, activations.dtype),
            pltpu.VMEM((depth // LANES, LANES), norm_gain.dtype),
            pltpu.VMEM((depth, columns), jnp.bfloat16),
            pltpu.SemaphoreType.DMA((2,)),
            pltpu.SemaphoreType.DMA((chunks,)),
        ],
        compiler_params=pltpu.CompilerParams(vmem_limit_bytes=12 << 20),
        name="project",
    )(*in_hbm(activations, norm_gain.reshape(-1, LANES), w_query))

    pick, gather, bias = pl.pallas_call(
        owners_kernel,
        out_shape=(
            jax.ShapeDtypeStruct((kv_heads, slots * group, group * rows), jnp.bfloat16),
            jax.ShapeDtypeStruct((kv_heads, group * rows, slots * group), jnp.bfloat16),
            jax.ShapeDtypeStruct((kv_heads, slots * group, group * rows), jnp.float32),
        ),
        in_specs=[pl.BlockSpec(memory_space=pl.ANY)] + [HBM] * 3,
        out_specs=(VMEM, VMEM, VMEM),
        scratch_shapes=[
            pltpu.VMEM(block_list.shape, block_list.dtype),
            pltpu.VMEM(block_slot_table.shape, block_slot_table.dtype),
            pltpu.VMEM(kept_len.shape[::-1], kept_len.dtype),
            pltpu.SemaphoreType.DMA((3,)),
        ],
        compiler_params=pltpu.CompilerParams(vmem_limit_bytes=8 << 20),
        cost_estimate=pl.CostEstimate(flops=0, bytes_accessed=4 << 20, transcendentals=0),
        name="owners",
    )(payload, *in_hbm(block_list, block_slot_table, kept_len.T))

    if lenders > DIRECT_MOST:
        parts = [lax.psum(payload, "lender")]
    else:
        parts = send_all(payload, "lender")

    tiles = state_blocks(kv_heads * group)[1]
    partial_state = pl.pallas_call(
        functools.partial(attend_kernel, parts=len(parts), width=depth * lenders),
        out_shape=jax.ShapeDtypeStruct((rows, columns + tiles * LANES), jnp.bfloat16),
        in_specs=[VMEM] * (len(parts) + 5),
        out_specs=VMEM,
        compiler_params=pltpu.CompilerParams(vmem_limit_bytes=24 << 20),
        name="attend",
    )(*parts, pick, gather, bias, key_pool, value_block_store)

    parts = send_all(partial_state, "lender")

    home = rows // peers
    sums = pl.pallas_call(
        functools.partial(output_kernel, parts=len(parts), peers=peers, head_dim=head_dim),
        out_shape=[jax.ShapeDtypeStruct((home, w_out.shape[1]), jnp.float32)] * peers,
        in_specs=[VMEM] * (len(parts) + 1),
        out_specs=[VMEM] * peers,
        compiler_params=pltpu.CompilerParams(vmem_limit_bytes=24 << 20),
        name="output",
    )(*parts, w_out)

    result = sums[0]
    for s in range(peers - 1, 0, -1):
        result = result + lax.ppermute(sums[s], "tensor", [(i, i ^ s) for i in range(peers)])
    return result.astype(jnp.bfloat16)


def solution(mesh):
    in_specs = (
        P("group", "lender"),
        P("lender"),
        P("lender", "tensor"),
        P("tensor", "lender"),
        P("tensor", ("group", "lender"), None, None),
        P("tensor", ("group", "lender"), None, None),
        P("group", "tensor", None),
        P("tensor", "group"),
        P("group", "tensor"),
    )
    out_specs = P(("group", "tensor"), "lender")
    return jax.shard_map(
        per_device, mesh=mesh, in_specs=in_specs, out_specs=out_specs, check_vma=False
    )
```

time: 31.8 us -> 30.2 us (0.950)
  Pallas kernels: 13.2 us -> 8.08 us
  waiting for transfers between devices: 4.39 us -> 9.2 us
  starting transfers between devices: 13.2 us -> 12.1 us
    pallas_call x2 -> x1, Pallas kernels: 5.7 us -> 1.15 us  [per_device(): pl.pallas_call(owners_kernel, out_shape=(jax.ShapeDtypeStruct((kv_heads,...]
    ppermute x6, waiting for transfers between devices: 2.95 us -> 7.28 us  [send_all(): return [value] + [lax.ppermute(value, axis, table) for table in tables]]
    ppermute x3, starting transfers between devices: 2.96 us -> 1.87 us  [per_device(): lax.ppermute(sums[s], 'tensor', [(i, i ^ s) for i in range(peers)])]
    pallas_call x1, Pallas kernels: 2.1 us -> 1.38 us  [per_device(): pl.pallas_call(functools.partial(attend_kernel, parts=len(parts), width=d...]
    ppermute x3, waiting for transfers between devices: 1.44 us -> 1.92 us  [per_device(): lax.ppermute(sums[s], 'tensor', [(i, i ^ s) for i in range(peers)])]
  transfers between devices with their start and end apart: 9 -> 9, of which waited for: 4 -> 6; matrix products, arithmetic and copies ran while one was open for 0% -> 0% of each run, Pallas kernels for 18% -> 4%
where the time goes in v4:
time: 30.2 us; the launch traced here: 30 us
  starting transfers between devices  12.1 us (40%)
  waiting for transfers between devices  9.2 us (30%)
  Pallas kernels  8.08 us (27%)
  other arithmetic  0.62 us (2%)
    ppermute x6, starting transfers between devices, send_all(): return [value] + [lax.ppermute(value, axis, table) for table in tables]  10.2 us
    ppermute x6, waiting for transfers between devices, send_all(): return [value] + [lax.ppermute(value, axis, table) for table in tables]  7.28 us
    pallas_call x1, Pallas kernels, per_device(): pl.pallas_call(project_kernel, out_shape=jax.ShapeDtypeStruct((rows, colu...  4.2 us
    ppermute x3, waiting for transfers between devices, per_device(): lax.ppermute(sums[s], 'tensor', [(i, i ^ s) for i in range(peers)])  1.92 us
    ppermute x3, starting transfers between devices, per_device(): lax.ppermute(sums[s], 'tensor', [(i, i ^ s) for i in range(peers)])  1.87 us
    pallas_call x1, Pallas kernels, per_device(): pl.pallas_call(functools.partial(attend_kernel, parts=len(parts), width=d...  1.38 us
    pallas_call x1, Pallas kernels, per_device(): pl.pallas_call(functools.partial(output_kernel, parts=len(parts), peers=p...  1.34 us
    pallas_call x1, Pallas kernels, per_device(): pl.pallas_call(owners_kernel, out_shape=(jax.ShapeDtypeStruct((kv_heads,...  1.15 us
  transfers between devices with their start and end apart: 9, of which 6 were waited for; matrix products, arithmetic and copies ran while one was open for 0% of the time, Pallas kernels for 4%

profile of v4, /device:TPU:0, one launch (start us, length us, event | category | flops | bytes accessed | tf_op | source)
XLA Modules:
  0.0 30.0 jit_solution(17958790321893861352)
XLA Ops:
  0.0 0.0 copy-start.2
  0.0 0.0 copy-start.1
  0.0 0.0 copy-start
  0.0 4.2 %project.1.after_hbm.refs_0_ = f32[8,2176]{1,0:T(8,128)S(1)} custom-call(bf16[8,2048]{1,0:T(8,128)(2,1)} %act_hbm.1, bf16[16,128]{1,0:T(8,128)(2,1)} %bitcast.2, bf16[2048,2048]{1,0:T(8,128)(2,1)} %w_hbm.1), custom_call_target="tpu_custom_call" | custom-call | tf_op jit(solution)/shard_map/project/pallas_call | solution.py:342
  4.2 5.1 %collective-permute-start.2 = (f32[8,2176]{1,0:T(8,128)S(1)}, f32[8,2176]{1,0:T(8,128)S(1)}, u32[]{:S(2)}, u32[]{:S(2)}) collective-permute-start(f32[8,2176]{1,0:T(8,128)S(1)} %project.1.after_hbm.refs_0_), channel_id=1, source_target_pairs={{0,12},{4,8},{8,4},{12,0},{1,13},{5,9},{9,5},{13,1},{2,14},{6,10},... | collective-permute-start | bytes 208904 | tf_op jit(solution)/shard_map/ppermute | solution.py:320
  9.4 0.0 collective-permute-start.1
  9.4 0.6 %collective-permute-start = (f32[8,2176]{1,0:T(8,128)S(1)}, f32[8,2176]{1,0:T(8,128)S(1)}, u32[]{:S(2)}, u32[]{:S(2)}) collective-permute-start(f32[8,2176]{1,0:T(8,128)S(1)} %project.1.after_hbm.refs_0_), channel_id=1, source_target_pairs={{0,4},{4,0},{8,12},{12,8},{1,5},{5,1},{9,13},{13,9},{2,6},{6,2},{1... | collective-permute-start | bytes 208904 | tf_op jit(solution)/shard_map/ppermute | solution.py:320
  10.0 1.2 %owners.1 = (bf16[2,256,64]{2,1,0:T(8,128)(2,1)S(1)}, bf16[2,64,256]{2,1,0:T(8,128)(2,1)S(1)}, f32[2,256,64]{2,1,0:T(8,128)S(1)}) custom-call(f32[8,2176]{1,0:T(8,128)S(1)} %project.1.after_hbm.refs_0_, s32[8,2,16]{2,1,0:T(2,128)} %list_hbm.1, s32[2,128]{1,0:T(2,128)} %table_hbm.1, s32[2,8]{1,0:T(2,128)} %bitcast.3), custom_call_target="tpu_custom_call" | custom-call | bytes 4194304 | tf_op jit(solution)/shard_map/owners/pallas_call | solution.py:358
  11.2 0.8 %collective-permute-done.2.refs_3_ = f32[8,2176]{1,0:T(8,128)S(1)} collective-permute-done((f32[8,2176]{1,0:T(8,128)S(1)}, f32[8,2176]{1,0:T(8,128)S(1)}, u32[]{:S(2)}, u32[]{:S(2)}) %collective-permute-start.2) | collective-permute-done | bytes 69664 | tf_op jit(solution)/shard_map/ppermute | solution.py:320
  11.9 3.3 %collective-permute-done.1.refs_2_ = f32[8,2176]{1,0:T(8,128)S(1)} collective-permute-done((f32[8,2176]{1,0:T(8,128)S(1)}, f32[8,2176]{1,0:T(8,128)S(1)}, u32[]{:S(2)}, u32[]{:S(2)}) %collective-permute-start.1) | collective-permute-done | bytes 69664 | tf_op jit(solution)/shard_map/ppermute | solution.py:320
  15.3 0.0 collective-permute-done.refs_1_
  15.3 0.0 copy-done.2
  15.3 0.0 copy-done.1
  15.3 1.4 %attend.1.refs_0_ = bf16[8,2176]{1,0:T(8,128)(2,1)S(1)} custom-call(f32[8,2176]{1,0:T(8,128)S(1)} %project.1.after_hbm.refs_0_, f32[8,2176]{1,0:T(8,128)S(1)} %collective-permute-done.refs_1_, f32[8,2176]{1,0:T(8,128)S(1)} %collective-permute-done.1.refs_2_, f32[8,2176]{1,0:T(8,128)S(1)} %collective-permute-done.2.refs_3_, ...), custom_call_target="tpu_custom_call" | custom-call | tf_op jit(solution)/shard_map/attend/pallas_call | solution.py:384
  16.7 2.7 %collective-permute-start.5 = (bf16[8,2176]{1,0:T(8,128)(2,1)S(1)}, bf16[8,2176]{1,0:T(8,128)(2,1)S(1)}, u32[]{:S(2)}, u32[]{:S(2)}) collective-permute-start(bf16[8,2176]{1,0:T(8,128)(2,1)S(1)} %attend.1.refs_0_), channel_id=1, source_target_pairs={{0,12},{4,8},{8,4},{12,0},{1,13},{5,9},{9,5},{13,1},{2,14},{6,10},... | collective-permute-start | bytes 104456 | tf_op jit(solution)/shard_map/ppermute | solution.py:320
  19.4 0.0 collective-permute-start.4
  19.4 1.7 %collective-permute-start.3 = (bf16[8,2176]{1,0:T(8,128)(2,1)S(1)}, bf16[8,2176]{1,0:T(8,128)(2,1)S(1)}, u32[]{:S(2)}, u32[]{:S(2)}) collective-permute-start(bf16[8,2176]{1,0:T(8,128)(2,1)S(1)} %attend.1.refs_0_), channel_id=1, source_target_pairs={{0,4},{4,0},{8,12},{12,8},{1,5},{5,1},{9,13},{13,9},{2,6},{6,2},{1... | collective-permute-start | bytes 104456 | tf_op jit(solution)/shard_map/ppermute | solution.py:320
  21.1 1.4 %collective-permute-done.5.refs_3_ = bf16[8,2176]{1,0:T(8,128)(2,1)S(1)} collective-permute-done((bf16[8,2176]{1,0:T(8,128)(2,1)S(1)}, bf16[8,2176]{1,0:T(8,128)(2,1)S(1)}, u32[]{:S(2)}, u32[]{:S(2)}) %collective-permute-start.5) | collective-permute-done | bytes 34848 | tf_op jit(solution)/shard_map/ppermute | solution.py:320
  22.5 1.7 %collective-permute-done.4.refs_2_ = bf16[8,2176]{1,0:T(8,128)(2,1)S(1)} collective-permute-done((bf16[8,2176]{1,0:T(8,128)(2,1)S(1)}, bf16[8,2176]{1,0:T(8,128)(2,1)S(1)}, u32[]{:S(2)}, u32[]{:S(2)}) %collective-permute-start.4) | collective-permute-done | bytes 34848 | tf_op jit(solution)/shard_map/ppermute | solution.py:320
  24.3 0.0 collective-permute-done.3.refs_1_
  24.3 0.0 copy-done
  24.3 1.3 %output.1 = (f32[2,2048]{1,0:T(2,128)S(1)}, f32[2,2048]{1,0:T(2,128)S(1)}, f32[2,2048]{1,0:T(2,128)S(1)}, f32[2,2048]{1,0:T(2,128)S(1)}) custom-call(bf16[8,2176]{1,0:T(8,128)(2,1)S(1)} %attend.1.refs_0_, bf16[8,2176]{1,0:T(8,128)(2,1)S(1)} %collective-permute-done.3.refs_1_, bf16[8,2176]{1,0:T(8,128)(2,1)S(1)} %collective-permute-done.4.refs_2_, ...), custom_call_target="tpu_custom_call" | custom-call | tf_op jit(solution)/shard_map/output/pallas_call | solution.py:396
  25.6 0.0 collective-permute-start.6
  25.6 1.5 %collective-permute-start.7 = (f32[2,2048]{1,0:T(2,128)S(1)}, f32[2,2048]{1,0:T(2,128)S(1)}, u32[]{:S(2)}, u32[]{:S(2)}) collective-permute-start(f32[2,2048]{1,0:T(2,128)S(1)} %get-tuple-element.17), channel_id=1, source_target_pairs={{0,2},{1,3},{2,0},{3,1},{4,6},{5,7},{6,4},{7,5},{8,10},{9,11},{10,... | collective-permute-start | bytes 49160 | tf_op jit(solution)/shard_map/ppermute | solution.py:407
  27.1 0.3 %collective-permute-start.8 = (f32[2,2048]{1,0:T(2,128)S(1)}, f32[2,2048]{1,0:T(2,128)S(1)}, u32[]{:S(2)}, u32[]{:S(2)}) collective-permute-start(f32[2,2048]{1,0:T(2,128)S(1)} %get-tuple-element.18), channel_id=1, source_target_pairs={{0,1},{1,0},{2,3},{3,2},{4,5},{5,4},{6,7},{7,6},{8,9},{9,8},{10,11... | collective-permute-start | bytes 49160 | tf_op jit(solution)/shard_map/ppermute | solution.py:407
  27.5 1.4 %collective-permute-done.6 = f32[2,2048]{1,0:T(2,128)S(1)} collective-permute-done((f32[2,2048]{1,0:T(2,128)S(1)}, f32[2,2048]{1,0:T(2,128)S(1)}, u32[]{:S(2)}, u32[]{:S(2)}) %collective-permute-start.6) | collective-permute-done | bytes 16416 | tf_op jit(solution)/shard_map/ppermute | solution.py:407
  28.9 0.5 %collective-permute-done.7 = f32[2,2048]{1,0:T(2,128)S(1)} collective-permute-done((f32[2,2048]{1,0:T(2,128)S(1)}, f32[2,2048]{1,0:T(2,128)S(1)}, u32[]{:S(2)}, u32[]{:S(2)}) %collective-permute-start.7) | collective-permute-done | bytes 16416 | tf_op jit(solution)/shard_map/ppermute | solution.py:407
  29.4 0.0 collective-permute-done.8
  29.4 0.6 %add_convert_fusion = bf16[2,2048]{1,0:T(2,128)(2,1)} fusion(f32[2,2048]{1,0:T(2,128)S(1)} %collective-permute-done.8, f32[2,2048]{1,0:T(2,128)S(1)} %collective-permute-done.7, f32[2,2048]{1,0:T(2,128)S(1)} %get-tuple-element.15, f32[2,2048]{1,0:T(2,128)S(1)} %collective-permute-done.6), kind=kLoop, calls=%fused_computation | loop fusion | flops 16384 | bytes 73728 | tf_op jit(solution)/shard_map/convert_element_type | solution.py:408
Async XLA Ops:
  0.0 15.3 %copy-start.2 = (bf16[2,32,128,128]{3,2,1,0:T(8,128)(2,1)S(1)}, bf16[2,32,128,128]{3,2,1,0:T(8,128)(2,1)}, u32[]{:S(2)}) copy-start(bf16[2,32,128,128]{3,2,1,0:T(8,128)(2,1)} %refs_8_.1) | copy-start | bytes 6291460
  0.0 15.3 %copy-start.1 = (bf16[2,32,128,128]{3,2,1,0:T(8,128)(2,1)S(1)}, bf16[2,32,128,128]{3,2,1,0:T(8,128)(2,1)}, u32[]{:S(2)}) copy-start(bf16[2,32,128,128]{3,2,1,0:T(8,128)(2,1)} %refs_7_.1) | copy-start | bytes 6291460
  0.0 24.3 %copy-start = (bf16[2048,2048]{1,0:T(8,128)(2,1)S(1)}, bf16[2048,2048]{1,0:T(8,128)(2,1)}, u32[]{:S(2)}) copy-start(bf16[2048,2048]{1,0:T(8,128)(2,1)} %refs_4_.1) | copy-start | bytes 25165828
  4.2 7.7 %collective-permute-start.2 = (f32[8,2176]{1,0:T(8,128)S(1)}, f32[8,2176]{1,0:T(8,128)S(1)}, u32[]{:S(2)}, u32[]{:S(2)}) collective-permute-start(f32[8,2176]{1,0:T(8,128)S(1)} %project.1.after_hbm.refs_0_), channel_id=1, source_target_pairs={{0,12},{4,8},{8,4},{12,0},{1,13},{5,9},{9,5},{13,1},{2,14},{6,10},... | collective-permute-start | bytes 208904 | tf_op jit(solution)/shard_map/ppermute | solution.py:320
  9.4 5.9 %collective-permute-start.1 = (f32[8,2176]{1,0:T(8,128)S(1)}, f32[8,2176]{1,0:T(8,128)S(1)}, u32[]{:S(2)}, u32[]{:S(2)}) collective-permute-start(f32[8,2176]{1,0:T(8,128)S(1)} %project.1.after_hbm.refs_0_), channel_id=1, source_target_pairs={{0,8},{4,12},{8,0},{12,4},{1,9},{5,13},{9,1},{13,5},{2,10},{6,14},... | collective-permute-start | bytes 208904 | tf_op jit(solution)/shard_map/ppermute | solution.py:320
  9.4 5.9 %collective-permute-start = (f32[8,2176]{1,0:T(8,128)S(1)}, f32[8,2176]{1,0:T(8,128)S(1)}, u32[]{:S(2)}, u32[]{:S(2)}) collective-permute-start(f32[8,2176]{1,0:T(8,128)S(1)} %project.1.after_hbm.refs_0_), channel_id=1, source_target_pairs={{0,4},{4,0},{8,12},{12,8},{1,5},{5,1},{9,13},{13,9},{2,6},{6,2},{1... | collective-permute-start | bytes 208904 | tf_op jit(solution)/shard_map/ppermute | solution.py:320
  16.7 5.9 %collective-permute-start.5 = (bf16[8,2176]{1,0:T(8,128)(2,1)S(1)}, bf16[8,2176]{1,0:T(8,128)(2,1)S(1)}, u32[]{:S(2)}, u32[]{:S(2)}) collective-permute-start(bf16[8,2176]{1,0:T(8,128)(2,1)S(1)} %attend.1.refs_0_), channel_id=1, source_target_pairs={{0,12},{4,8},{8,4},{12,0},{1,13},{5,9},{9,5},{13,1},{2,14},{6,10},... | collective-permute-start | bytes 104456 | tf_op jit(solution)/shard_map/ppermute | solution.py:320
  19.4 4.8 %collective-permute-start.4 = (bf16[8,2176]{1,0:T(8,128)(2,1)S(1)}, bf16[8,2176]{1,0:T(8,128)(2,1)S(1)}, u32[]{:S(2)}, u32[]{:S(2)}) collective-permute-start(bf16[8,2176]{1,0:T(8,128)(2,1)S(1)} %attend.1.refs_0_), channel_id=1, source_target_pairs={{0,8},{4,12},{8,0},{12,4},{1,9},{5,13},{9,1},{13,5},{2,10},{6,14},... | collective-permute-start | bytes 104456 | tf_op jit(solution)/shard_map/ppermute | solution.py:320
  19.4 4.8 %collective-permute-start.3 = (bf16[8,2176]{1,0:T(8,128)(2,1)S(1)}, bf16[8,2176]{1,0:T(8,128)(2,1)S(1)}, u32[]{:S(2)}, u32[]{:S(2)}) collective-permute-start(bf16[8,2176]{1,0:T(8,128)(2,1)S(1)} %attend.1.refs_0_), channel_id=1, source_target_pairs={{0,4},{4,0},{8,12},{12,8},{1,5},{5,1},{9,13},{13,9},{2,6},{6,2},{1... | collective-permute-start | bytes 104456 | tf_op jit(solution)/shard_map/ppermute | solution.py:320
  25.6 3.3 %collective-permute-start.6 = (f32[2,2048]{1,0:T(2,128)S(1)}, f32[2,2048]{1,0:T(2,128)S(1)}, u32[]{:S(2)}, u32[]{:S(2)}) collective-permute-start(f32[2,2048]{1,0:T(2,128)S(1)} %get-tuple-element.16), channel_id=1, source_target_pairs={{0,3},{1,2},{2,1},{3,0},{4,7},{5,6},{6,5},{7,4},{8,11},{9,10},{10,... | collective-permute-start | bytes 49160 | tf_op jit(solution)/shard_map/ppermute | solution.py:407
  25.6 3.8 %collective-permute-start.7 = (f32[2,2048]{1,0:T(2,128)S(1)}, f32[2,2048]{1,0:T(2,128)S(1)}, u32[]{:S(2)}, u32[]{:S(2)}) collective-permute-start(f32[2,2048]{1,0:T(2,128)S(1)} %get-tuple-element.17), channel_id=1, source_target_pairs={{0,2},{1,3},{2,0},{3,1},{4,6},{5,7},{6,4},{7,5},{8,10},{9,11},{10,... | collective-permute-start | bytes 49160 | tf_op jit(solution)/shard_map/ppermute | solution.py:407
  27.1 2.3 %collective-permute-start.8 = (f32[2,2048]{1,0:T(2,128)S(1)}, f32[2,2048]{1,0:T(2,128)S(1)}, u32[]{:S(2)}, u32[]{:S(2)}) collective-permute-start(f32[2,2048]{1,0:T(2,128)S(1)} %get-tuple-element.18), channel_id=1, source_target_pairs={{0,1},{1,0},{2,3},{3,2},{4,5},{5,4},{6,7},{7,6},{8,9},{9,8},{10,11... | collective-permute-start | bytes 49160 | tf_op jit(solution)/shard_map/ppermute | solution.py:407
